TPU v7x, 256 devices: a whole 4x4x8 slice. The times are simulated.
256 devices in a mesh: aa: 4 (over x), ba: 8 (over z), col: 8 (over y, core).
Axes of the slice: x: 4, y: 4, z: 8, core: 2. Of those that a mesh axis runs over, the one named last changes fastest.
Arguments:
- tensor: bfloat16 [1024, 1024, 1024], P('aa', 'ba', 'col'), may hold values from -6 to 6
- factor_two: bfloat16 [1024, 64], P('ba'), may hold values from -0.1875 to 0.1875
- factor_three: bfloat16 [1024, 64], P('col'), may hold values from -0.1875 to 0.1875
Outputs:
- gram: float32 [1024, 1024], P('aa', ('ba', 'col'))
All inputs are finite; a program needn't handle non-finite values.
Results may differ from a plain program's by a relative error of at most 0.008.
Values sent between devices are 32-bit elements; how exact they have to be, the bound alone decides.
A program may use at most 64 MiB of HBM per device.

v0:
```python
import jax
import jax.numpy as jnp
from jax import lax
from jax.sharding import PartitionSpec as P


def body(tensor, factor_two, factor_three):
    rank = factor_three.shape[1]
    local_rows = tensor.shape[0]
    local_two = tensor.shape[1]
    partial_value = jnp.einsum(
        "ijk,ks->jsi", tensor, factor_three, preferred_element_type=jnp.float32
    ).astype(jnp.bfloat16)
    flat_partial = partial_value.reshape(local_two, rank * local_rows)
    n_mid = lax.axis_size("ba")
    n_last = lax.axis_size("col")
    width = min(
        rank,
        (rank * rank // (n_mid * n_last) * lax.axis_size(("ba", "col")) + rank - 1) // rank + 1,
    )
    product = jnp.dot(factor_two.T, flat_partial, preferred_element_type=jnp.float32)
    product = product.reshape(width * rank, local_rows)
    columns_here = lax.psum_scatter(product, ("ba", "col"), scatter_dimension=0, tiled=True)
    scale = 1.0 / (rank * rank)
    gram_terms = jnp.dot(
        columns_here.T,
        lax.all_gather(columns_here, "aa", axis=1, tiled=True),
        precision=lax.Precision.HIGHEST,
        preferred_element_type=jnp.float32,
    )
    gram = lax.psum_scatter(gram_terms, ("ba", "col"), scatter_dimension=1, tiled=True) * scale
    return gram


def solution(mesh):
    return jax.shard_map(
        body,
        mesh=mesh,
        in_specs=(P("aa", "ba", "col"), P("ba", None), P("col", None)),
        out_specs=P("aa", ("ba", "col")),
        check_vma=False,
    )
```

profile of v0, /device:TPU:1, one launch (start us, length us, event | category | flops | bytes accessed | tf_op | source)
XLA Modules:
  0.0 328.4 jit_solution(15639007261280793211)
XLA Ops:
  6.5 0.0 copy-start
  6.5 0.0 reduce-scatter.3.cloned.1.call-start
  6.5 0.7 copy-done
  7.3 6.4 %convert_bitcast_fusion = bf16[128,64,256]{0,1,2:T(8,128)(2,1)S(1)} fusion(bf16[256,128,128]{2,1,0:T(8,128)(2,1)} %param.3, bf16[128,64]{0,1:T(8,128)(2,1)S(1)} %copy-done), kind=kOutput, calls=%fused_computation.1 | convolution fusion | flops 538968064 | bytes 12599296 | tf_op jit(solution)/shard_map/ijk,ks->jsi/dot_general | solution.py:11
  13.7 0.0 copy-start.1
  13.7 2.7 copy.4
  16.4 0.0 copy-done.1
  16.4 3.5 %convolution_bitcast_fusion = f32[64,16384]{1,0:T(8,128)} fusion(bf16[128,16384]{0,1:T(8,128)(2,1)S(1)} %bitcast.13, bf16[128,64]{0,1:T(8,128)(2,1)S(1)} %copy-done.1), kind=kOutput, calls=%fused_computation | convolution fusion | flops 268435456 | bytes 8404992 | tf_op jit(solution)/shard_map/dot_general | solution.py:21
  19.9 4.9 %reshape.7 = f32[4096,256]{1,0:T(8,128)} reshape(f32[64,16384]{1,0:T(8,128)} %convolution_bitcast_fusion) | data formatting | bytes 8388608 | tf_op jit(solution)/shard_map/reshape | solution.py:22
  24.8 0.0 reduce-scatter.3.cloned.1.call-update
  24.8 0.0 reduce-scatter.5.cloned.1.call-start
  24.9 142.4 %reduce-scatter.3.cloned.1.call-done = f32[64,256]{1,0:T(8,128)} async-done(((f32[4096,256]{1,0:T(8,128)}), f32[64,256]{1,0:T(8,128)}) %reduce-scatter.3.cloned.1.call-update) | async-done | bytes 65552 | tf_op jit(solution)/shard_map/reduce_scatter | solution.py:23
  167.2 10.0 %all_gather.3 = f32[64,1024]{1,0:T(8,128)S(1)} all-gather(f32[64,256]{1,0:T(8,128)} %reduce-scatter.3.cloned.1.call-done), channel_id=1, replica_groups=mesh['aa'=4,'ba'=8,'col'=8] {'aa'}, dimensions={1}, use_global_device_ids=true | all-gather | bytes 327680 | tf_op jit(solution)/shard_map/all_gather | solution.py:27
  177.2 2.8 fusion.1
  180.0 0.0 reduce-scatter.5.cloned.1.call-update
  180.1 140.2 %reduce-scatter.5.cloned.1.call-done = f32[256,16]{0,1:T(8,128)} async-done(((f32[256,1024]{0,1:T(8,128)}), f32[256,16]{0,1:T(8,128)}) %reduce-scatter.5.cloned.1.call-update) | async-done | bytes 16400 | tf_op jit(solution)/shard_map/reduce_scatter | solution.py:31
  320.2 1.3 broadcast_multiply_fusion
Async XLA Ops:
  6.5 0.7 copy-start
  6.5 160.7 %reduce-scatter.3.cloned.1.call-start = ((), (), s32[]{:S(2)}) async-start(), calls=%async_computation.2 | async-start | bytes 4259840 | tf_op jit(solution)/shard_map/reduce_scatter | solution.py:23
  13.7 2.7 copy-start.1
  24.8 295.4 %reduce-scatter.5.cloned.1.call-start = ((), (), s32[]{:S(2)}) async-start(), calls=%async_computation.3 | async-start | bytes 1064960 | tf_op jit(solution)/shard_map/reduce_scatter | solution.py:31
Sparse Core Ops, SparseCore 0:
  24.9 142.2 reduce-scatter.2
  180.2 139.9 reduce-scatter.4
where the time goes:
time: 333 us; the launch traced here: 328 us
  waiting for transfers between devices  283 us (85%)
  between operations  13.4 us (4%)
  matrix products  12.8 us (4%)
  blocking collectives  9.97 us (3%)
  local copies, waits for them, and re-layouts  8.29 us (2%)
    reduce_scatter x1, waiting for transfers between devices, body(): lax.psum_scatter(product, ('ba', 'col'), scatter_dimension=0, tiled=True)  142 us
    reduce_scatter x1, waiting for transfers between devices, body(): lax.psum_scatter(gram_terms, ('ba', 'col'), scatter_dimension=1, tiled=True)  140 us
    all_gather x1, blocking collectives, body(): lax.all_gather(columns_here, 'aa', axis=1, tiled=True)  9.97 us
  transfers between devices with their start and end apart: 2, of which 2 were waited for; matrix products, arithmetic and copies ran while one was open for 0% of the time, Pallas kernels for 0%

commit v1 on v0

v1 whole, which is shorter than its diff:
```python
import jax
import jax.numpy as jnp
from jax import lax
from jax.sharding import PartitionSpec as P


def project(tensor, factor_two, factor_three):
    rank = factor_three.shape[1]
    local_rows = tensor.shape[0]
    local_two = tensor.shape[1]
    partial_value = jnp.einsum(
        "ijk,ks->jsi", tensor, factor_three, preferred_element_type=jnp.float32
    ).astype(jnp.bfloat16)
    flat_partial = partial_value.reshape(local_two, rank * local_rows)
    product = jnp.dot(factor_two.T, flat_partial, preferred_element_type=jnp.float32)
    return product.reshape(rank * rank, local_rows)


def a2a_rs(x, axis):
    n = lax.axis_size(axis)
    parts = x.reshape(n, x.shape[0] // n, *x.shape[1:])
    got = lax.all_to_all(parts, axis, 0, 0, tiled=False)
    return got.sum(axis=0)


def body(tensor, factor_two, factor_three):
    rank = factor_three.shape[1]
    product = project(tensor, factor_two, factor_three)
    columns_here = a2a_rs(a2a_rs(product, "col"), "ba")
    gathered = lax.all_gather(columns_here, "aa", axis=1, tiled=True)
    terms = jnp.dot(gathered.T, columns_here, precision=lax.Precision.HIGHEST, preferred_element_type=jnp.float32)
    gram_t = a2a_rs(a2a_rs(terms, "ba"), "col")
    return gram_t.T * (1.0 / (rank * rank))


def solution(mesh):
    return jax.shard_map(
        body,
        mesh=mesh,
        in_specs=(P("aa", "ba", "col"), P("ba", None), P("col", None)),
        out_specs=P("aa", ("ba", "col")),
        check_vma=False,
    )
```

time: 333 us -> 152 us (0.46); the launches traced: 328 us -> 152 us
  waiting for transfers between devices: 283 us -> 0 us
  blocking collectives: 9.97 us -> 129 us
  between operations: 13.4 us -> 0.05 us
    reduce_scatter x2 -> x0, waiting for transfers between devices: 283 us -> none  [the longest x1 142 us: body(): lax.psum_scatter(product, ('ba', 'col'), scatter_dimension=0, tiled=True)]
    all_to_all x0 -> x4, blocking collectives: none -> 120 us  [a2a_rs(): got = lax.all_to_all(parts, axis, 0, 0, tiled=False)]
    reshape x1 -> x0, local copies, waits for them, and re-layouts: 4.87 us -> none  [body(): product = product.reshape(width * rank, local_rows)]
    another operation x0 -> x1, local copies, waits for them, and re-layouts: none -> 4.87 us  [a2a_rs(): parts = x.reshape(n, x.shape[0] // n, *x.shape[1:])]
  transfers between devices with their start and end apart: 2 -> 0, of which waited for: 2 -> 0; matrix products, arithmetic and copies ran while one was open for 0% -> 0% of each run, Pallas kernels for 0% -> 0%
where the time goes in v1:
time: 152 us
  blocking collectives  129 us (85%)
  matrix products  11 us (7%)
  local copies, waits for them, and re-layouts  8.3 us (5%)
  other arithmetic  3.24 us (2%)
    all_to_all x4, blocking collectives, a2a_rs(): got = lax.all_to_all(parts, axis, 0, 0, tiled=False)  120 us
    all_gather x1, blocking collectives, body(): gathered = lax.all_gather(columns_here, 'aa', axis=1, tiled=True)  9.73 us
    dot_general x1, matrix products, project(): jnp.einsum('ijk,ks->jsi', tensor, factor_three, preferred_element_type=jn...  6.39 us
    another operation x1, local copies, waits for them, and re-layouts, a2a_rs(): parts = x.reshape(n, x.shape[0] // n, *x.shape[1:])  4.87 us
    dot_general x1, matrix products, project(): jnp.dot(factor_two.T, flat_partial, preferred_element_type=jnp.float32)  3.54 us

profile of v1, /device:TPU:1, one launch (start us, length us, event | category | flops | bytes accessed | tf_op | source)
XLA Modules:
  0.0 152.0 jit_solution(414881436349180238)
XLA Ops:
  0.0 0.0 copy-start
  0.0 0.7 copy-done
  0.7 6.4 %convert_bitcast_fusion = bf16[128,64,256]{0,1,2:T(8,128)(2,1)S(1)} fusion(bf16[256,128,128]{2,1,0:T(8,128)(2,1)} %param.3, bf16[128,64]{0,1:T(8,128)(2,1)S(1)} %copy-done), kind=kOutput, calls=%fused_computation.1 | convolution fusion | flops 538968064 | bytes 12599296 | tf_op jit(solution)/shard_map/ijk,ks->jsi/dot_general | solution.py:11
  7.1 0.0 copy-start.1
  7.1 2.7 %copy.6 = bf16[128,64,256]{0,2,1:T(8,128)(2,1)S(1)} copy(bf16[128,64,256]{0,1,2:T(8,128)(2,1)S(1)} %convert_bitcast_fusion) | data formatting | bytes 8388608 | tf_op jit(solution)/shard_map/convert_element_type | solution.py:13
  9.8 0.0 copy-done.1
  9.9 3.5 %convolution_bitcast_fusion = f32[64,16384]{1,0:T(8,128)} fusion(bf16[128,16384]{0,1:T(8,128)(2,1)S(1)} %bitcast.26, bf16[128,64]{0,1:T(8,128)(2,1)S(1)} %copy-done.1), kind=kOutput, calls=%fused_computation | convolution fusion | flops 268435456 | bytes 8404992 | tf_op jit(solution)/shard_map/dot_general | solution.py:15
  13.4 4.9 %reshape_reshape.3 = f32[8,512,256]{2,1,0:T(8,128)} reshape(f32[64,16384]{1,0:T(8,128)} %convolution_bitcast_fusion) | data formatting | bytes 8388608 | tf_op jit(solution)/shard_map/reshape;reshape | solution.py:21
  18.3 57.0 %all_to_all.20 = f32[8,512,256]{2,1,0:T(8,128)} all-to-all(f32[8,512,256]{2,1,0:T(8,128)} %reshape_reshape.3), channel_id=1, replica_groups=mesh['aa'=4,'ba'=8,'col'=8] {'col'}, dimensions={0} | all-to-all | bytes 8388608 | tf_op jit(solution)/shard_map/all_to_all | solution.py:22
  75.3 2.5 %reduce_sum.36 = f32[512,256]{1,0:T(8,128)S(1)} reduce(f32[8,512,256]{2,1,0:T(8,128)} %all_to_all.20, f32[]{:T(128)} %constant.0.clone.1), dimensions={0}, to_apply=%region_0.0 | reduce | flops 917504 | bytes 4718596 | tf_op jit(solution)/shard_map/reduce_sum | solution.py:23
  77.8 21.9 %all_to_all.21 = f32[8,64,256]{2,1,0:T(8,128)S(1)} all-to-all(f32[8,64,256]{2,1,0:T(8,128)S(1)} %bitcast.27), channel_id=1, replica_groups=mesh['aa'=4,'ba'=8,'col'=8] {'ba'}, dimensions={0} | all-to-all | bytes 1048576 | tf_op jit(solution)/shard_map/all_to_all | solution.py:22
  99.7 9.7 %all_gather.3 = f32[64,1024]{1,0:T(8,128)S(1)} all-gather(f32[64,256]{1,0:T(8,128)S(1)} %reduce_sum.37), channel_id=1, replica_groups=mesh['aa'=4,'ba'=8,'col'=8] {'aa'}, dimensions={1}, use_global_device_ids=true | all-gather | bytes 327680 | tf_op jit(solution)/shard_map/all_gather | solution.py:30
  109.4 1.0 fusion
  110.5 26.5 %all_to_all.22 = f32[8,128,256]{2,1,0:T(8,128)S(1)} all-to-all(f32[8,128,256]{2,1,0:T(8,128)S(1)} %fusion), channel_id=1, replica_groups=mesh['aa'=4,'ba'=8,'col'=8] {'ba'}, dimensions={0} | all-to-all | bytes 2097152 | tf_op jit(solution)/shard_map/all_to_all | solution.py:22
  136.9 0.1 reduce_sum.38
  137.0 14.4 %all_to_all.23 = f32[8,16,256]{2,1,0:T(8,128)S(1)} all-to-all(f32[8,16,256]{2,1,0:T(8,128)S(1)} %bitcast.28), channel_id=1, replica_groups=mesh['aa'=4,'ba'=8,'col'=8] {'col'}, dimensions={0} | all-to-all | bytes 262144 | tf_op jit(solution)/shard_map/all_to_all | solution.py:22
  151.4 0.6 multiply_bitcast_fusion
  (2 shorter events, 0.0 us)
Async XLA Ops:
  0.0 0.7 copy-start
  7.1 2.7 %copy-start.1 = (bf16[128,64]{0,1:T(8,128)(2,1)S(1)}, bf16[128,64]{0,1:T(8,128)(2,1)}, u32[]{:S(2)}) copy-start(bf16[128,64]{0,1:T(8,128)(2,1)} %param.4) | copy-start | bytes 49156

commit v2 on v1

--- a/solution.py
+++ b/solution.py
@@ -1,7 +1,78 @@
+import functools
+
 import jax
 import jax.numpy as jnp
 from jax import lax
+from jax.experimental import pallas as pl
+from jax.experimental.pallas import tpu as pltpu
 from jax.sharding import PartitionSpec as P
+
+MESH = pl.DeviceIdType.MESH
+
+
+def ring_kernel(axis, n, x_ref, out_ref, recv, sendbuf, send_sem, recv_sem):
+    me = lax.axis_index(axis)
+    right = lax.rem(me + 1, n)
+    left = lax.rem(me + n - 1, n)
+    half = x_ref.shape[1] // 2
+    lanes = (pl.ds(0, half), pl.ds(half, half))
+    towards = (right, left)
+
+    barrier = pltpu.get_barrier_semaphore()
+    for neighbour in (left, right):
+        pl.semaphore_signal(barrier, inc=1, device_id={axis: neighbour}, device_id_type=MESH)
+    pl.semaphore_wait(barrier, 2)
+
+    def chunk_sent(d, step):
+        return lax.rem(me - step - 1 + 2 * n, n) if d == 0 else lax.rem(me + step + 1, n)
+
+    for step in range(n - 1):
+        copies = []
+        for d in range(2):
+            if step == 0:
+                src = x_ref.at[chunk_sent(d, 0), lanes[d]]
+            else:
+                src = sendbuf.at[d, step]
+            copy = pltpu.make_async_remote_copy(
+                src_ref=src,
+                dst_ref=recv.at[d, step],
+                send_sem=send_sem.at[d, step],
+                recv_sem=recv_sem.at[d, step],
+                device_id={axis: towards[d]},
+                device_id_type=MESH,
+            )
+            copy.start()
+            copies.append(copy)
+        for d in range(2):
+            copies[d].wait_recv()
+            got = chunk_sent(d, step + 1)
+            total = recv[d, step] + x_ref[got, lanes[d]]
+            if step < n - 2:
+                sendbuf[d, step + 1] = total
+            else:
+                out_ref[lanes[d]] = total
+        for d in range(2):
+            copies[d].wait_send()
+
+
+def ring_reduce_scatter(x, axis, n, collective_id):
+    rows = x.shape[0] // n
+    cols = x.shape[1]
+    half = rows // 2
+    parts = x.reshape(n, rows, cols)
+    return pl.pallas_call(
+        functools.partial(ring_kernel, axis, n),
+        out_shape=jax.ShapeDtypeStruct((rows, cols), x.dtype),
+        in_specs=[pl.BlockSpec(memory_space=pltpu.VMEM)],
+        out_specs=pl.BlockSpec(memory_space=pltpu.VMEM),
+        scratch_shapes=[
+            pltpu.VMEM((2, n - 1, half, cols), x.dtype),
+            pltpu.VMEM((2, n - 1, half, cols), x.dtype),
+            pltpu.SemaphoreType.DMA((2, n - 1)),
+            pltpu.SemaphoreType.DMA((2, n - 1)),
+        ],
+        compiler_params=pltpu.CompilerParams(collective_id=collective_id, has_side_effects=True),
+    )(parts)
 
 
 def project(tensor, factor_two, factor_three):
@@ -26,7 +97,7 @@
 def body(tensor, factor_two, factor_three):
     rank = factor_three.shape[1]
     product = project(tensor, factor_two, factor_three)
-    columns_here = a2a_rs(a2a_rs(product, "col"), "ba")
+    columns_here = a2a_rs(ring_reduce_scatter(product, "col", lax.axis_size("col"), 0), "ba")
     gathered = lax.all_gather(columns_here, "aa", axis=1, tiled=True)
     terms = jnp.dot(gathered.T, columns_here, precision=lax.Precision.HIGHEST, preferred_element_type=jnp.float32)
     gram_t = a2a_rs(a2a_rs(terms, "ba"), "col")

time: 152 us -> 139 us (0.914)
  blocking collectives: 129 us -> 76.6 us
  Pallas kernels: 0 us -> 41.7 us
  other arithmetic: 3.24 us -> 0.72 us
    all_to_all x4 -> x3, blocking collectives: 120 us -> 66.6 us  [a2a_rs(): got = lax.all_to_all(parts, axis, 0, 0, tiled=False)]
    pallas_call x0 -> x1, Pallas kernels: none -> 41.7 us  [ring_reduce_scatter(): pl.pallas_call(functools.partial(ring_kernel, axis, n), out_shape=jax.Sha...]
    reduce_sum x4 -> x3, other arithmetic: 2.63 us -> 0.11 us  [a2a_rs(): return got.sum(axis=0)]
where the time goes in v2:
time: 139 us; the launch traced here: 138 us
  blocking collectives  76.6 us (55%)
  Pallas kernels  41.7 us (30%)
  matrix products  11 us (8%)
  local copies, waits for them, and re-layouts  8.3 us (6%)
    all_to_all x3, blocking collectives, a2a_rs(): got = lax.all_to_all(parts, axis, 0, 0, tiled=False)  66.6 us
    pallas_call x1, Pallas kernels, ring_reduce_scatter(): pl.pallas_call(functools.partial(ring_kernel, axis, n), out_shape=jax.Sha...  41.7 us
    all_gather x1, blocking collectives, body(): gathered = lax.all_gather(columns_here, 'aa', axis=1, tiled=True)  10 us
    dot_general x1, matrix products, project(): jnp.einsum('ijk,ks->jsi', tensor, factor_three, preferred_element_type=jn...  6.39 us
    another operation x1, local copies, waits for them, and re-layouts, ring_reduce_scatter(): parts = x.reshape(n, rows, cols)  4.87 us
    dot_general x1, matrix products, project(): jnp.dot(factor_two.T, flat_partial, preferred_element_type=jnp.float32)  3.54 us

profile of v2, /device:TPU:1, one launch (start us, length us, event | category | flops | bytes accessed | tf_op | source)
XLA Modules:
  0.0 138.4 jit_solution(9693446261434462100)
XLA Ops:
  0.0 0.0 copy-start
  0.0 0.7 copy-done
  0.7 6.4 %convert_bitcast_fusion = bf16[128,64,256]{0,1,2:T(8,128)(2,1)S(1)} fusion(bf16[256,128,128]{2,1,0:T(8,128)(2,1)} %param.3, bf16[128,64]{0,1:T(8,128)(2,1)S(1)} %copy-done), kind=kOutput, calls=%fused_computation.1 | convolution fusion | flops 538968064 | bytes 12599296 | tf_op jit(solution)/shard_map/ijk,ks->jsi/dot_general | solution.py:82
  7.1 0.0 copy-start.1
  7.1 2.7 %copy.6 = bf16[128,64,256]{0,2,1:T(8,128)(2,1)S(1)} copy(bf16[128,64,256]{0,1,2:T(8,128)(2,1)S(1)} %convert_bitcast_fusion) | data formatting | bytes 8388608 | tf_op jit(solution)/shard_map/convert_element_type | solution.py:84
  9.8 0.0 copy-done.1
  9.9 3.5 %convolution_bitcast_fusion = f32[64,16384]{1,0:T(8,128)} fusion(bf16[128,16384]{0,1:T(8,128)(2,1)S(1)} %bitcast.26, bf16[128,64]{0,1:T(8,128)(2,1)S(1)} %copy-done.1), kind=kOutput, calls=%fused_computation | convolution fusion | flops 268435456 | bytes 8404992 | tf_op jit(solution)/shard_map/dot_general | solution.py:86
  13.4 4.9 %reshape_reshape.3.x_ref = f32[8,512,256]{2,1,0:T(8,128)} reshape(f32[64,16384]{1,0:T(8,128)} %convolution_bitcast_fusion) | data formatting | bytes 8388608 | tf_op jit(solution)/shard_map/reshape;reshape | solution.py:62
  18.3 41.7 %shard_map.37 = f32[512,256]{1,0:T(8,128)} custom-call(f32[8,512,256]{2,1,0:T(8,128)} %reshape_reshape.3.x_ref), custom_call_target="tpu_custom_call" | custom-call | tf_op jit(solution)/shard_map/pallas_call | solution.py:63
  60.0 21.2 %all_to_all.15 = f32[8,64,256]{2,1,0:T(8,128)S(1)} all-to-all(f32[8,64,256]{2,1,0:T(8,128)} %bitcast.27), channel_id=1, replica_groups=mesh['aa'=4,'ba'=8,'col'=8] {'ba'}, dimensions={0} | all-to-all | bytes 1048576 | tf_op jit(solution)/shard_map/all_to_all | solution.py:93
  81.3 10.0 %all_gather.3 = f32[64,1024]{1,0:T(8,128)S(1)} all-gather(f32[64,256]{1,0:T(8,128)S(1)} %reduce_sum.27), channel_id=1, replica_groups=mesh['aa'=4,'ba'=8,'col'=8] {'aa'}, dimensions={1}, use_global_device_ids=true | all-gather | bytes 327680 | tf_op jit(solution)/shard_map/all_gather | solution.py:101
  91.3 1.0 fusion
  92.3 24.6 %all_to_all.16 = f32[8,128,256]{2,1,0:T(8,128)S(1)} all-to-all(f32[8,128,256]{2,1,0:T(8,128)S(1)} %fusion), channel_id=1, replica_groups=mesh['aa'=4,'ba'=8,'col'=8] {'ba'}, dimensions={0} | all-to-all | bytes 2097152 | tf_op jit(solution)/shard_map/all_to_all | solution.py:93
  116.9 0.1 reduce_sum.28
  117.0 20.8 %all_to_all.17 = f32[8,16,256]{2,1,0:T(8,128)S(1)} all-to-all(f32[8,16,256]{2,1,0:T(8,128)S(1)} %bitcast.28), channel_id=1, replica_groups=mesh['aa'=4,'ba'=8,'col'=8] {'col'}, dimensions={0} | all-to-all | bytes 262144 | tf_op jit(solution)/shard_map/all_to_all | solution.py:93
  137.7 0.6 multiply_bitcast_fusion
  (2 shorter events, 0.0 us)
Async XLA Ops:
  0.0 0.7 copy-start
  7.1 2.7 %copy-start.1 = (bf16[128,64]{0,1:T(8,128)(2,1)S(1)}, bf16[128,64]{0,1:T(8,128)(2,1)}, u32[]{:S(2)}) copy-start(bf16[128,64]{0,1:T(8,128)(2,1)} %param.4) | copy-start | bytes 49156

commit v3 on v2

--- a/solution.py
+++ b/solution.py
@@ -75,6 +75,169 @@
     )(parts)
 
 
+def group_index(axes, sizes):
+    flat = lax.axis_index(axes[0])
+    for axis, size in zip(axes[1:], sizes[1:]):
+        flat = flat * size + lax.axis_index(axis)
+    return flat
+
+
+def group_device(axes, sizes, flat):
+    place = {}
+    for axis, size in reversed(list(zip(axes, sizes))):
+        place[axis] = lax.rem(flat, size)
+        flat = flat // size
+    return place
+
+
+def greet_all(axes, sizes, n, me):
+    barrier = pltpu.get_barrier_semaphore()
+
+    def greet(peer, carry):
+        @pl.when(peer != me)
+        def _():
+            pl.semaphore_signal(barrier, inc=1, device_id=group_device(axes, sizes, peer), device_id_type=MESH)
+        return carry
+
+    lax.fori_loop(0, n, greet, 0)
+    pl.semaphore_wait(barrier, n - 1)
+
+
+def direct_rs_kernel(axes, sizes, x_ref, out_ref, recv, send_sem, recv_sem):
+    n = x_ref.shape[0]
+    me = group_index(axes, sizes)
+    greet_all(axes, sizes, n, me)
+
+    def outgoing(peer):
+        return pltpu.make_async_remote_copy(
+            src_ref=x_ref.at[peer],
+            dst_ref=recv.at[me],
+            send_sem=send_sem.at[peer],
+            recv_sem=recv_sem.at[me],
+            device_id=group_device(axes, sizes, peer),
+            device_id_type=MESH,
+        )
+
+    def incoming(peer):
+        return pltpu.make_async_remote_copy(
+            src_ref=x_ref.at[me],
+            dst_ref=recv.at[peer],
+            send_sem=send_sem.at[peer],
+            recv_sem=recv_sem.at[peer],
+            device_id=group_device(axes, sizes, peer),
+            device_id_type=MESH,
+        )
+
+    def start(step, carry):
+        peer = lax.rem(me + step, n)
+        outgoing(peer).start()
+        return carry
+
+    lax.fori_loop(1, n, start, 0)
+    out_ref[...] = x_ref[me]
+
+    def gather(step, carry):
+        peer = lax.rem(me + n - step, n)
+        incoming(peer).wait_recv()
+        out_ref[...] += recv[peer]
+        return carry
+
+    lax.fori_loop(1, n, gather, 0)
+
+    def finish(step, carry):
+        peer = lax.rem(me + step, n)
+        outgoing(peer).wait_send()
+        return carry
+
+    lax.fori_loop(1, n, finish, 0)
+
+
+def direct_reduce_scatter(x, axes, sizes, collective_id):
+    n = 1
+    for size in sizes:
+        n *= size
+    rows = x.shape[0] // n
+    cols = x.shape[1]
+    parts = x.reshape(n, rows, cols)
+    return pl.pallas_call(
+        functools.partial(direct_rs_kernel, tuple(axes), tuple(sizes)),
+        out_shape=jax.ShapeDtypeStruct((rows, cols), x.dtype),
+        in_specs=[pl.BlockSpec(memory_space=pltpu.VMEM)],
+        out_specs=pl.BlockSpec(memory_space=pltpu.VMEM),
+        scratch_shapes=[
+            pltpu.VMEM((n, rows, cols), x.dtype),
+            pltpu.SemaphoreType.DMA((n,)),
+            pltpu.SemaphoreType.DMA((n,)),
+        ],
+        compiler_params=pltpu.CompilerParams(collective_id=collective_id, has_side_effects=True),
+    )(parts)
+
+
+def direct_gather_kernel(axes, sizes, x_ref, out_ref, recv, send_sem, recv_sem):
+    n = recv.shape[0]
+    me = group_index(axes, sizes)
+    greet_all(axes, sizes, n, me)
+
+    def outgoing(peer):
+        return pltpu.make_async_remote_copy(
+            src_ref=x_ref,
+            dst_ref=recv.at[me],
+            send_sem=send_sem.at[peer],
+            recv_sem=recv_sem.at[me],
+            device_id=group_device(axes, sizes, peer),
+            device_id_type=MESH,
+        )
+
+    def incoming(peer):
+        return pltpu.make_async_remote_copy(
+            src_ref=x_ref,
+            dst_ref=recv.at[peer],
+            send_sem=send_sem.at[peer],
+            recv_sem=recv_sem.at[peer],
+            device_id=group_device(axes, sizes, peer),
+            device_id_type=MESH,
+        )
+
+    def start(step, carry):
+        outgoing(lax.rem(me + step, n)).start()
+        return carry
+
+    lax.fori_loop(1, n, start, 0)
+    out_ref[me] = x_ref[...]
+
+    def gather(step, carry):
+        peer = lax.rem(me + n - step, n)
+        incoming(peer).wait_recv()
+        out_ref[peer] = recv[peer]
+        return carry
+
+    lax.fori_loop(1, n, gather, 0)
+
+    def finish(step, carry):
+        outgoing(lax.rem(me + step, n)).wait_send()
+        return carry
+
+    lax.fori_loop(1, n, finish, 0)
+
+
+def direct_all_gather(x, axes, sizes, collective_id):
+    n = 1
+    for size in sizes:
+        n *= size
+    return pl.pallas_call(
+        functools.partial(direct_gather_kernel, tuple(axes), tuple(sizes)),
+        out_shape=jax.ShapeDtypeStruct((n, *x.shape), x.dtype),
+        in_specs=[pl.BlockSpec(memory_space=pltpu.VMEM)],
+        out_specs=pl.BlockSpec(memory_space=pltpu.VMEM),
+        scratch_shapes=[
+            pltpu.VMEM((n, *x.shape), x.dtype),
+            pltpu.SemaphoreType.DMA((n,)),
+            pltpu.SemaphoreType.DMA((n,)),
+        ],
+        compiler_params=pltpu.CompilerParams(collective_id=collective_id, has_side_effects=True),
+    )(x)
+
+
 def project(tensor, factor_two, factor_three):
     rank = factor_three.shape[1]
     local_rows = tensor.shape[0]
@@ -97,10 +260,12 @@
 def body(tensor, factor_two, factor_three):
     rank = factor_three.shape[1]
     product = project(tensor, factor_two, factor_three)
-    columns_here = a2a_rs(ring_reduce_scatter(product, "col", lax.axis_size("col"), 0), "ba")
-    gathered = lax.all_gather(columns_here, "aa", axis=1, tiled=True)
-    terms = jnp.dot(gathered.T, columns_here, precision=lax.Precision.HIGHEST, preferred_element_type=jnp.float32)
-    gram_t = a2a_rs(a2a_rs(terms, "ba"), "col")
+    n_col, n_ba, n_aa = lax.axis_size("col"), lax.axis_size("ba"), lax.axis_size("aa")
+    columns_here = direct_reduce_scatter(ring_reduce_scatter(product, "col", n_col, 0), ("ba",), (n_ba,), 3)
+    gathered = direct_all_gather(columns_here, ("aa",), (n_aa,), 2)
+    terms = jnp.einsum("pmj,mi->pji", gathered, columns_here, precision=lax.Precision.HIGHEST, preferred_element_type=jnp.float32)
+    terms = terms.reshape(n_aa * columns_here.shape[1], columns_here.shape[1])
+    gram_t = direct_reduce_scatter(terms, ("ba", "col"), (n_ba, n_col), 1)
     return gram_t.T * (1.0 / (rank * rank))
 
 

time: 139 us -> 129 us (0.928)
  blocking collectives: 76.6 us -> 0 us
  Pallas kernels: 41.7 us -> 106 us
  matrix products: 11 us -> 12.9 us
    all_to_all x3 -> x0, blocking collectives: 66.6 us -> none  [a2a_rs(): got = lax.all_to_all(parts, axis, 0, 0, tiled=False)]
    pallas_call x0 -> x3, Pallas kernels: none -> 64.4 us  [the longest x2 56.6 us: direct_reduce_scatter(): pl.pallas_call(functools.partial(direct_rs_kernel, tuple(axes), tuple(siz...]
    all_gather x1 -> x0, blocking collectives: 10 us -> none  [body(): gathered = lax.all_gather(columns_here, 'aa', axis=1, tiled=True)]
    dot_general x1, matrix products: 1.03 us -> 2.95 us  [body(): jnp.einsum('pmj,mi->pji', gathered, columns_here, precision=lax.Precision...]
where the time goes in v3:
time: 129 us
  Pallas kernels  106 us (82%)
  matrix products  12.9 us (10%)
  local copies, waits for them, and re-layouts  8.29 us (6%)
  other arithmetic  1.33 us (1%)
    pallas_call x2, Pallas kernels, direct_reduce_scatter(): pl.pallas_call(functools.partial(direct_rs_kernel, tuple(axes), tuple(siz...  56.6 us
    pallas_call x1, Pallas kernels, ring_reduce_scatter(): pl.pallas_call(functools.partial(ring_kernel, axis, n), out_shape=jax.Sha...  41.7 us
    pallas_call x1, Pallas kernels, direct_all_gather(): pl.pallas_call(functools.partial(direct_gather_kernel, tuple(axes), tuple...  7.81 us
    dot_general x1, matrix products, project(): jnp.einsum('ijk,ks->jsi', tensor, factor_three, preferred_element_type=jn...  6.39 us
    another operation x1, local copies, waits for them, and re-layouts, ring_reduce_scatter(): parts = x.reshape(n, rows, cols)  4.87 us
    dot_general x1, matrix products, project(): jnp.dot(factor_two.T, flat_partial, preferred_element_type=jnp.float32)  3.53 us
    dot_general x1, matrix products, body(): jnp.einsum('pmj,mi->pji', gathered, columns_here, precision=lax.Precision...  2.95 us
    convert_element_type x1, local copies, waits for them, and re-layouts, project(): partial_value = jnp.einsum('ijk,ks->jsi', tensor, factor_three, preferred...  2.7 us

profile of v3, /device:TPU:1, one launch (start us, length us, event | category | flops | bytes accessed | tf_op | source)
XLA Modules:
  0.0 128.7 jit_solution(6190215843497017866)
XLA Ops:
  0.0 0.0 copy-start
  0.0 0.7 copy-done
  0.7 6.4 %convert_bitcast_fusion = bf16[128,64,256]{0,1,2:T(8,128)(2,1)S(1)} fusion(bf16[256,128,128]{2,1,0:T(8,128)(2,1)} %param.3, bf16[128,64]{0,1:T(8,128)(2,1)S(1)} %copy-done), kind=kOutput, calls=%fused_computation.1 | convolution fusion | flops 538968064 | bytes 12599296 | tf_op jit(solution)/shard_map/ijk,ks->jsi/dot_general | solution.py:245
  7.1 0.0 copy-start.1
  7.1 2.7 %copy.4 = bf16[128,64,256]{0,2,1:T(8,128)(2,1)S(1)} copy(bf16[128,64,256]{0,1,2:T(8,128)(2,1)S(1)} %convert_bitcast_fusion) | data formatting | bytes 8388608 | tf_op jit(solution)/shard_map/convert_element_type | solution.py:247
  9.8 0.0 copy-done.1
  9.9 3.5 %convolution_bitcast_fusion = f32[64,16384]{1,0:T(8,128)} fusion(bf16[128,16384]{0,1:T(8,128)(2,1)S(1)} %bitcast.19, bf16[128,64]{0,1:T(8,128)(2,1)S(1)} %copy-done.1), kind=kOutput, calls=%fused_computation | convolution fusion | flops 268435456 | bytes 8404992 | tf_op jit(solution)/shard_map/dot_general | solution.py:249
  13.4 4.9 %reshape_reshape.6.x_ref = f32[8,512,256]{2,1,0:T(8,128)} reshape(f32[64,16384]{1,0:T(8,128)} %convolution_bitcast_fusion) | data formatting | bytes 8388608 | tf_op jit(solution)/shard_map/reshape;reshape | solution.py:62
  18.2 41.7 %shard_map.37 = f32[512,256]{1,0:T(8,128)} custom-call(f32[8,512,256]{2,1,0:T(8,128)} %reshape_reshape.6.x_ref), custom_call_target="tpu_custom_call" | custom-call | tf_op jit(solution)/shard_map/pallas_call | solution.py:63
  60.0 18.6 %shard_map.38.x_ref = f32[64,256]{1,0:T(8,128)} custom-call(f32[8,64,256]{2,1,0:T(8,128)} %bitcast.21), custom_call_target="tpu_custom_call" | custom-call | tf_op jit(solution)/shard_map/pallas_call | solution.py:162
  78.6 7.8 %shard_map.39 = f32[4,64,256]{2,1,0:T(8,128)} custom-call(f32[64,256]{1,0:T(8,128)} %shard_map.38.x_ref), custom_call_target="tpu_custom_call" | custom-call | tf_op jit(solution)/shard_map/pallas_call | solution.py:227
  86.4 3.0 %fusion = f32[4,256,256]{2,1,0:T(8,128)} fusion(f32[4,64,256]{2,1,0:T(8,128)} %shard_map.39, f32[64,256]{1,0:T(8,128)} %shard_map.38.x_ref), kind=kOutput, calls=%fused_computation.2 | convolution fusion | flops 201326592 | bytes 1376256 | tf_op jit(solution)/shard_map/pmj,mi->pji/dot_general | solution.py:266
  89.4 38.0 %shard_map.40 = f32[16,256]{1,0:T(8,128)} custom-call(f32[64,16,256]{2,1,0:T(8,128)} %bitcast.20), custom_call_target="tpu_custom_call" | custom-call | tf_op jit(solution)/shard_map/pallas_call | solution.py:162
  127.4 1.3 %multiply_bitcast_fusion = f32[256,16]{0,1:T(8,128)} fusion(f32[16,256]{1,0:T(8,128)} %shard_map.40), kind=kLoop, calls=%fused_computation.5 | loop fusion | flops 4096 | bytes 32768 | tf_op jit(solution)/shard_map/mul | solution.py:269
Async XLA Ops:
  0.0 0.7 copy-start
  7.1 2.7 %copy-start.1 = (bf16[128,64]{0,1:T(8,128)(2,1)S(1)}, bf16[128,64]{0,1:T(8,128)(2,1)}, u32[]{:S(2)}) copy-start(bf16[128,64]{0,1:T(8,128)(2,1)} %param.4) | copy-start | bytes 49156

commit v4 on v3

--- a/solution.py
+++ b/solution.py
@@ -250,30 +250,35 @@
     return product.reshape(rank * rank, local_rows)
 
 
-def a2a_rs(x, axis):
-    n = lax.axis_size(axis)
-    parts = x.reshape(n, x.shape[0] // n, *x.shape[1:])
-    got = lax.all_to_all(parts, axis, 0, 0, tiled=False)
-    return got.sum(axis=0)
-
-
 def body(tensor, factor_two, factor_three):
     rank = factor_three.shape[1]
     product = project(tensor, factor_two, factor_three)
-    n_col, n_ba, n_aa = lax.axis_size("col"), lax.axis_size("ba"), lax.axis_size("aa")
-    columns_here = direct_reduce_scatter(ring_reduce_scatter(product, "col", n_col, 0), ("ba",), (n_ba,), 3)
+    n_core, n_y, n_ba, n_aa = lax.axis_size("core"), lax.axis_size("y"), lax.axis_size("ba"), lax.axis_size("aa")
+    n_col = n_core * n_y
+    on_chip = direct_reduce_scatter(product, ("core",), (n_core,), 5)
+    columns_here = direct_reduce_scatter(ring_reduce_scatter(on_chip, "y", n_y, 0), ("ba",), (n_ba,), 3)
     gathered = direct_all_gather(columns_here, ("aa",), (n_aa,), 2)
-    terms = jnp.einsum("pmj,mi->pji", gathered, columns_here, precision=lax.Precision.HIGHEST, preferred_element_type=jnp.float32)
-    terms = terms.reshape(n_aa * columns_here.shape[1], columns_here.shape[1])
-    gram_t = direct_reduce_scatter(terms, ("ba", "col"), (n_ba, n_col), 1)
+    depth, rows = columns_here.shape
+    per_block = n_ba // n_aa
+    out_rows = rows * n_aa // (n_ba * n_col)
+    ordered = gathered.reshape(n_aa, depth, per_block, n_col, out_rows).transpose(3, 0, 2, 4, 1)
+    terms = jnp.einsum("cpbtm,mi->cpbti", ordered, columns_here, precision=lax.Precision.HIGHEST, preferred_element_type=jnp.float32)
+    terms = terms.reshape(n_col * n_ba * out_rows, rows)
+    gram_t = direct_reduce_scatter(terms, ("y", "core"), (n_y, n_core), 1)
+    gram_t = direct_reduce_scatter(gram_t, ("ba",), (n_ba,), 4)
     return gram_t.T * (1.0 / (rank * rank))
 
 
 def solution(mesh):
+    n_core = 2
+    shape = mesh.devices.shape
+    split = jax.sharding.Mesh(
+        mesh.devices.reshape(shape[0], shape[1], shape[2] // n_core, n_core), ("aa", "ba", "y", "core")
+    )
     return jax.shard_map(
         body,
-        mesh=mesh,
-        in_specs=(P("aa", "ba", "col"), P("ba", None), P("col", None)),
-        out_specs=P("aa", ("ba", "col")),
+        mesh=split,
+        in_specs=(P("aa", "ba", ("y", "core")), P("ba", None), P(("y", "core"), None)),
+        out_specs=P("aa", ("ba", "y", "core")),
         check_vma=False,
     )

time: 129 us -> 117 us (0.907)
  Pallas kernels: 106 us -> 92.4 us
    pallas_call x1, Pallas kernels: 41.7 us -> 23.9 us  [ring_reduce_scatter(): pl.pallas_call(functools.partial(ring_kernel, axis, n), out_shape=jax.Sha...]
    pallas_call x2 -> x4, Pallas kernels: 56.6 us -> 60.7 us  [direct_reduce_scatter(): pl.pallas_call(functools.partial(direct_rs_kernel, tuple(axes), tuple(siz...]
where the time goes in v4:
time: 117 us; the launch traced here: 116 us
  Pallas kernels  92.4 us (79%)
  matrix products  12.7 us (11%)
  local copies, waits for them, and re-layouts  9.44 us (8%)
  other arithmetic  1.33 us (1%)
    pallas_call x4, Pallas kernels, direct_reduce_scatter(): pl.pallas_call(functools.partial(direct_rs_kernel, tuple(axes), tuple(siz...  60.7 us
    pallas_call x1, Pallas kernels, ring_reduce_scatter(): pl.pallas_call(functools.partial(ring_kernel, axis, n), out_shape=jax.Sha...  23.9 us
    pallas_call x1, Pallas kernels, direct_all_gather(): pl.pallas_call(functools.partial(direct_gather_kernel, tuple(axes), tuple...  7.77 us
    dot_general x1, matrix products, project(): jnp.einsum('ijk,ks->jsi', tensor, factor_three, preferred_element_type=jn...  6.39 us
    another operation x1, local copies, waits for them, and re-layouts, direct_reduce_scatter(): parts = x.reshape(n, rows, cols)  4.87 us
    dot_general x1, matrix products, project(): jnp.dot(factor_two.T, flat_partial, preferred_element_type=jnp.float32)  3.53 us
    dot_general x1, matrix products, body(): jnp.einsum('cpbtm,mi->cpbti', ordered, columns_here, precision=lax.Precis...  2.79 us
    convert_element_type x1, local copies, waits for them, and re-layouts, project(): partial_value = jnp.einsum('ijk,ks->jsi', tensor, factor_three, preferred...  2.7 us

profile of v4, /device:TPU:1, one launch (start us, length us, event | category | flops | bytes accessed | tf_op | source)
XLA Modules:
  0.0 115.9 jit_solution(10477255937731212504)
XLA Ops:
  0.0 0.0 copy-start
  0.0 0.7 copy-done
  0.7 6.4 %convert_bitcast_fusion = bf16[128,64,256]{0,1,2:T(8,128)(2,1)S(1)} fusion(bf16[256,128,128]{2,1,0:T(8,128)(2,1)} %param.3, bf16[128,64]{0,1:T(8,128)(2,1)S(1)} %copy-done), kind=kOutput, calls=%fused_computation.1 | convolution fusion | flops 538968064 | bytes 12599296 | tf_op jit(solution)/shard_map/ijk,ks->jsi/dot_general | solution.py:245
  7.1 0.0 copy-start.1
  7.1 2.7 %copy.5 = bf16[128,64,256]{0,2,1:T(8,128)(2,1)S(1)} copy(bf16[128,64,256]{0,1,2:T(8,128)(2,1)S(1)} %convert_bitcast_fusion) | data formatting | bytes 8388608 | tf_op jit(solution)/shard_map/convert_element_type | solution.py:247
  9.8 0.0 copy-done.1
  9.9 3.5 %convolution_bitcast_fusion = f32[64,16384]{1,0:T(8,128)} fusion(bf16[128,16384]{0,1:T(8,128)(2,1)S(1)} %bitcast.25, bf16[128,64]{0,1:T(8,128)(2,1)S(1)} %copy-done.1), kind=kOutput, calls=%fused_computation | convolution fusion | flops 268435456 | bytes 8404992 | tf_op jit(solution)/shard_map/dot_general | solution.py:249
  13.4 4.9 %reshape_reshape.6.x_ref = f32[2,2048,256]{2,1,0:T(8,128)} reshape(f32[64,16384]{1,0:T(8,128)} %convolution_bitcast_fusion) | data formatting | bytes 8388608 | tf_op jit(solution)/shard_map/reshape;reshape | solution.py:161
  18.2 10.6 %shard_map.37 = f32[2048,256]{1,0:T(8,128)} custom-call(f32[2,2048,256]{2,1,0:T(8,128)} %reshape_reshape.6.x_ref), custom_call_target="tpu_custom_call" | custom-call | tf_op jit(solution)/shard_map/pallas_call | solution.py:162
  28.9 23.9 %shard_map.38 = f32[512,256]{1,0:T(8,128)} custom-call(f32[4,512,256]{2,1,0:T(8,128)} %bitcast.26), custom_call_target="tpu_custom_call" | custom-call | tf_op jit(solution)/shard_map/pallas_call | solution.py:63
  52.8 19.3 %shard_map.39.x_ref = f32[64,256]{1,0:T(8,128)} custom-call(f32[8,64,256]{2,1,0:T(8,128)} %bitcast.29), custom_call_target="tpu_custom_call" | custom-call | tf_op jit(solution)/shard_map/pallas_call | solution.py:162
  72.1 7.8 %shard_map.40 = f32[4,64,256]{2,1,0:T(8,128)} custom-call(f32[64,256]{1,0:T(8,128)} %shard_map.39.x_ref), custom_call_target="tpu_custom_call" | custom-call | tf_op jit(solution)/shard_map/pallas_call | solution.py:227
  79.9 1.1 copy.6
  81.1 2.8 %fusion = f32[8,4,2,16,256]{4,3,2,1,0:T(8,128)} fusion(f32[8,4,2,16,64]{4,3,0,2,1:T(8,128)S(1)} %bitcast.28, f32[64,256]{1,0:T(8,128)} %shard_map.39.x_ref), kind=kOutput, calls=%fused_computation.2 | convolution fusion | flops 201326592 | bytes 1376256 | tf_op jit(solution)/shard_map/cpbtm,mi->cpbti/dot_general | solution.py:265
  83.9 20.8 %shard_map.41 = f32[128,256]{1,0:T(8,128)} custom-call(f32[8,128,256]{2,1,0:T(8,128)} %bitcast.27), custom_call_target="tpu_custom_call" | custom-call | tf_op jit(solution)/shard_map/pallas_call | solution.py:162
  104.7 9.9 %shard_map.42 = f32[16,256]{1,0:T(8,128)} custom-call(f32[8,16,256]{2,1,0:T(8,128)} %bitcast.30), custom_call_target="tpu_custom_call" | custom-call | tf_op jit(solution)/shard_map/pallas_call | solution.py:162
  114.6 1.3 %multiply_bitcast_fusion = f32[256,16]{0,1:T(8,128)} fusion(f32[16,256]{1,0:T(8,128)} %shard_map.42), kind=kLoop, calls=%fused_computation.6 | loop fusion | flops 4096 | bytes 32768 | tf_op jit(solution)/shard_map/mul | solution.py:269
Async XLA Ops:
  0.0 0.7 copy-start
  7.1 2.7 %copy-start.1 = (bf16[128,64]{0,1:T(8,128)(2,1)S(1)}, bf16[128,64]{0,1:T(8,128)(2,1)}, u32[]{:S(2)}) copy-start(bf16[128,64]{0,1:T(8,128)(2,1)} %param.4) | copy-start | bytes 49156

commit v5 on v4

--- a/solution.py
+++ b/solution.py
@@ -241,12 +241,10 @@
 def project(tensor, factor_two, factor_three):
     rank = factor_three.shape[1]
     local_rows = tensor.shape[0]
-    local_two = tensor.shape[1]
     partial_value = jnp.einsum(
-        "ijk,ks->jsi", tensor, factor_three, preferred_element_type=jnp.float32
+        "ijk,ks->ijs", tensor, factor_three, preferred_element_type=jnp.float32
     ).astype(jnp.bfloat16)
-    flat_partial = partial_value.reshape(local_two, rank * local_rows)
-    product = jnp.dot(factor_two.T, flat_partial, preferred_element_type=jnp.float32)
+    product = jnp.einsum("jr,ijs->sri", factor_two, partial_value, preferred_element_type=jnp.float32)
     return product.reshape(rank * rank, local_rows)
 
 

time: 117 us -> 112 us (0.957)
  local copies, waits for them, and re-layouts: 9.44 us -> 1.86 us
  matrix products: 12.7 us -> 15.5 us
    another operation x1 -> x0, local copies, waits for them, and re-layouts: 4.87 us -> none  [direct_reduce_scatter(): parts = x.reshape(n, rows, cols)]
    dot_general x2, matrix products: 9.92 us -> 12.7 us  [the longest x1 6.39 us: project(): jnp.einsum('ijk,ks->ijs', tensor, factor_three, preferred_element_type=jn...]
    convert_element_type x1 -> x0, local copies, waits for them, and re-layouts: 2.7 us -> none  [project(): partial_value = jnp.einsum('ijk,ks->jsi', tensor, factor_three, preferred...]
where the time goes in v5:
time: 112 us; the launch traced here: 111 us
  Pallas kernels  92.4 us (82%)
  matrix products  15.5 us (14%)
  local copies, waits for them, and re-layouts  1.86 us (2%)
  other arithmetic  1.33 us (1%)
    pallas_call x4, Pallas kernels, direct_reduce_scatter(): pl.pallas_call(functools.partial(direct_rs_kernel, tuple(axes), tuple(siz...  60.7 us
    pallas_call x1, Pallas kernels, ring_reduce_scatter(): pl.pallas_call(functools.partial(ring_kernel, axis, n), out_shape=jax.Sha...  23.9 us
    pallas_call x1, Pallas kernels, direct_all_gather(): pl.pallas_call(functools.partial(direct_gather_kernel, tuple(axes), tuple...  7.77 us
    dot_general x1, matrix products, project(): jnp.einsum('ijk,ks->ijs', tensor, factor_three, preferred_element_type=jn...  6.39 us
    dot_general x1, matrix products, project(): jnp.einsum('jr,ijs->sri', factor_two, partial_value, preferred_element_ty...  6.35 us
    dot_general x1, matrix products, body(): jnp.einsum('cpbtm,mi->cpbti', ordered, columns_here, precision=lax.Precis...  2.79 us

profile of v5, /device:TPU:1, one launch (start us, length us, event | category | flops | bytes accessed | tf_op | source)
XLA Modules:
  0.0 111.2 jit_solution(749464753122043845)
XLA Ops:
  0.0 0.0 copy-start
  0.0 0.0 copy-start.1
  0.0 0.7 copy-done
  0.7 6.4 %fusion.5 = bf16[256,128,64]{1,2,0:T(8,128)(2,1)S(1)} fusion(bf16[256,128,128]{2,1,0:T(8,128)(2,1)} %param.3, bf16[128,64]{0,1:T(8,128)(2,1)S(1)} %copy-done), kind=kOutput, calls=%fused_computation.6 | convolution fusion | flops 536870912 | bytes 12599296 | tf_op jit(solution)/shard_map/ijk,ks->ijs/dot_general | solution.py:244
  7.1 0.0 copy-done.1
  7.1 6.4 %fusion = f32[256,64,64]{0,2,1:T(8,128)} fusion(bf16[256,128,64]{1,2,0:T(8,128)(2,1)S(1)} %fusion.5, bf16[128,64]{0,1:T(8,128)(2,1)S(1)} %copy-done.1), kind=kOutput, calls=%fused_computation.1 | convolution fusion | flops 268435456 | bytes 8404992 | tf_op jit(solution)/shard_map/jr,ijs->sri/dot_general | solution.py:247
  13.5 10.6 %shard_map.37 = f32[2048,256]{1,0:T(8,128)} custom-call(f32[2,2048,256]{2,1,0:T(8,128)} %bitcast.24), custom_call_target="tpu_custom_call" | custom-call | tf_op jit(solution)/shard_map/pallas_call | solution.py:162
  24.1 23.9 %shard_map.38 = f32[512,256]{1,0:T(8,128)} custom-call(f32[4,512,256]{2,1,0:T(8,128)} %bitcast.25), custom_call_target="tpu_custom_call" | custom-call | tf_op jit(solution)/shard_map/pallas_call | solution.py:63
  48.0 19.3 %shard_map.39.x_ref = f32[64,256]{1,0:T(8,128)} custom-call(f32[8,64,256]{2,1,0:T(8,128)} %bitcast.28), custom_call_target="tpu_custom_call" | custom-call | tf_op jit(solution)/shard_map/pallas_call | solution.py:162
  67.3 7.8 %shard_map.40 = f32[4,64,256]{2,1,0:T(8,128)} custom-call(f32[64,256]{1,0:T(8,128)} %shard_map.39.x_ref), custom_call_target="tpu_custom_call" | custom-call | tf_op jit(solution)/shard_map/pallas_call | solution.py:227
  75.1 1.1 %copy.5 = f32[4,64,256]{1,2,0:T(8,128)S(1)} copy(f32[4,64,256]{2,1,0:T(8,128)} %shard_map.40) | data formatting | bytes 524288 | tf_op jit(solution)/shard_map/pallas_call | solution.py:227
  76.2 2.8 %fusion.1 = f32[8,4,2,16,256]{4,3,2,1,0:T(8,128)} fusion(f32[8,4,2,16,64]{4,3,0,2,1:T(8,128)S(1)} %bitcast.27, f32[64,256]{1,0:T(8,128)} %shard_map.39.x_ref), kind=kOutput, calls=%fused_computation.2 | convolution fusion | flops 201326592 | bytes 1376256 | tf_op jit(solution)/shard_map/cpbtm,mi->cpbti/dot_general | solution.py:263
  79.0 20.9 %shard_map.41 = f32[128,256]{1,0:T(8,128)} custom-call(f32[8,128,256]{2,1,0:T(8,128)} %bitcast.26), custom_call_target="tpu_custom_call" | custom-call | tf_op jit(solution)/shard_map/pallas_call | solution.py:162
  99.9 10.0 %shard_map.42 = f32[16,256]{1,0:T(8,128)} custom-call(f32[8,16,256]{2,1,0:T(8,128)} %bitcast.29), custom_call_target="tpu_custom_call" | custom-call | tf_op jit(solution)/shard_map/pallas_call | solution.py:162
  109.9 1.3 %multiply_bitcast_fusion = f32[256,16]{0,1:T(8,128)} fusion(f32[16,256]{1,0:T(8,128)} %shard_map.42), kind=kLoop, calls=%fused_computation.8 | loop fusion | flops 4096 | bytes 32768 | tf_op jit(solution)/shard_map/mul | solution.py:267
Async XLA Ops:
  0.0 0.7 copy-start
  0.0 7.1 %copy-start.1 = (bf16[128,64]{0,1:T(8,128)(2,1)S(1)}, bf16[128,64]{0,1:T(8,128)(2,1)}, u32[]{:S(2)}) copy-start(bf16[128,64]{0,1:T(8,128)(2,1)} %param.4) | copy-start | bytes 49156

commit v6 on v5

--- a/solution.py
+++ b/solution.py
@@ -238,6 +238,156 @@
     )(x)
 
 
+def gram_kernel(sizes, q_ref, qt_ref, out_ref, gath, terms, recv_col, part, recv_ba, sems):
+    n_aa, n_ba, n_y, n_core = sizes
+    n_col = n_y * n_core
+    per_block = n_ba // n_aa
+    out_rows = out_ref.shape[0]
+    send_g, recv_g, send_c, recv_c, send_b, recv_b = sems
+    me_aa = lax.axis_index("aa")
+    me_ba = lax.axis_index("ba")
+    me_col = lax.axis_index("y") * n_core + lax.axis_index("core")
+
+    def aa_dev(p):
+        return {"aa": p}
+
+    def col_dev(c):
+        return {"y": c // n_core, "core": lax.rem(c, n_core)}
+
+    def ba_dev(b):
+        return {"ba": b}
+
+    barrier = pltpu.get_barrier_semaphore()
+    groups = ((n_aa, me_aa, aa_dev), (n_col, me_col, col_dev), (n_ba, me_ba, ba_dev))
+    for n, me, dev in groups:
+        def greet(step, carry, n=n, me=me, dev=dev):
+            pl.semaphore_signal(barrier, inc=1, device_id=dev(lax.rem(me + step, n)), device_id_type=MESH)
+            return carry
+
+        lax.fori_loop(1, n, greet, 0)
+    pl.semaphore_wait(barrier, n_aa + n_col + n_ba - 3)
+
+    def copy(src, dst, send, recv, dev):
+        return pltpu.make_async_remote_copy(
+            src_ref=src, dst_ref=dst, send_sem=send, recv_sem=recv, device_id=dev, device_id_type=MESH
+        )
+
+    def g_out(p):
+        return copy(qt_ref, gath.at[me_aa], send_g.at[p], recv_g.at[me_aa], aa_dev(p))
+
+    def g_in(p):
+        return copy(qt_ref, gath.at[p], send_g.at[p], recv_g.at[p], aa_dev(p))
+
+    def g_start(step, carry):
+        g_out(lax.rem(me_aa + step, n_aa)).start()
+        return carry
+
+    lax.fori_loop(1, n_aa, g_start, 0)
+    gath[me_aa] = qt_ref[...]
+
+    def g_wait(step, carry):
+        g_in(lax.rem(me_aa + n_aa - step, n_aa)).wait_recv()
+        return carry
+
+    lax.fori_loop(1, n_aa, g_wait, 0)
+
+    q = q_ref[...]
+    for c in range(n_col):
+        pieces = []
+        for p in range(n_aa):
+            for b2 in range(per_block):
+                start = b2 * n_col * out_rows + c * out_rows
+                pieces.append(gath[p, start:start + out_rows, :])
+        lhs = jnp.concatenate(pieces, axis=0)
+        block = jnp.dot(lhs, q, precision=lax.Precision.HIGHEST, preferred_element_type=jnp.float32)
+        terms[c] = block.reshape(n_ba, out_rows, q.shape[1])
+
+    def g_done(step, carry):
+        g_out(lax.rem(me_aa + step, n_aa)).wait_send()
+        return carry
+
+    lax.fori_loop(1, n_aa, g_done, 0)
+
+    def c_out(c):
+        return copy(terms.at[c], recv_col.at[me_col], send_c.at[c], recv_c.at[me_col], col_dev(c))
+
+    def c_in(c):
+        return copy(terms.at[c], recv_col.at[c], send_c.at[c], recv_c.at[c], col_dev(c))
+
+    def c_start(step, carry):
+        c_out(lax.rem(me_col + step, n_col)).start()
+        return carry
+
+    lax.fori_loop(1, n_col, c_start, 0)
+    part[...] = terms[me_col]
+
+    def c_wait(step, carry):
+        peer = lax.rem(me_col + n_col - step, n_col)
+        c_in(peer).wait_recv()
+        part[...] += recv_col[peer]
+        return carry
+
+    lax.fori_loop(1, n_col, c_wait, 0)
+
+    def b_out(b):
+        return copy(part.at[b], recv_ba.at[me_ba], send_b.at[b], recv_b.at[me_ba], ba_dev(b))
+
+    def b_in(b):
+        return copy(part.at[b], recv_ba.at[b], send_b.at[b], recv_b.at[b], ba_dev(b))
+
+    def b_start(step, carry):
+        b_out(lax.rem(me_ba + step, n_ba)).start()
+        return carry
+
+    lax.fori_loop(1, n_ba, b_start, 0)
+
+    def c_done(step, carry):
+        c_out(lax.rem(me_col + step, n_col)).wait_send()
+        return carry
+
+    lax.fori_loop(1, n_col, c_done, 0)
+    out_ref[...] = part[me_ba]
+
+    def b_wait(step, carry):
+        peer = lax.rem(me_ba + n_ba - step, n_ba)
+        b_in(peer).wait_recv()
+        out_ref[...] += recv_ba[peer]
+        return carry
+
+    lax.fori_loop(1, n_ba, b_wait, 0)
+
+    def b_done(step, carry):
+        b_out(lax.rem(me_ba + step, n_ba)).wait_send()
+        return carry
+
+    lax.fori_loop(1, n_ba, b_done, 0)
+
+
+def gram_reduce(q, sizes, collective_id):
+    n_aa, n_ba, n_y, n_core = sizes
+    n_col = n_y * n_core
+    depth, rows = q.shape
+    out_rows = rows * n_aa // (n_ba * n_col)
+    f32 = jnp.float32
+    return pl.pallas_call(
+        functools.partial(gram_kernel, sizes),
+        out_shape=jax.ShapeDtypeStruct((out_rows, rows), f32),
+        in_specs=[pl.BlockSpec(memory_space=pltpu.VMEM)] * 2,
+        out_specs=pl.BlockSpec(memory_space=pltpu.VMEM),
+        scratch_shapes=[
+            pltpu.VMEM((n_aa, rows, depth), f32),
+            pltpu.VMEM((n_col, n_ba, out_rows, rows), f32),
+            pltpu.VMEM((n_col, n_ba, out_rows, rows), f32),
+            pltpu.VMEM((n_ba, out_rows, rows), f32),
+            pltpu.VMEM((n_ba, out_rows, rows), f32),
+            [pltpu.SemaphoreType.DMA((n_aa,)), pltpu.SemaphoreType.DMA((n_aa,)),
+             pltpu.SemaphoreType.DMA((n_col,)), pltpu.SemaphoreType.DMA((n_col,)),
+             pltpu.SemaphoreType.DMA((n_ba,)), pltpu.SemaphoreType.DMA((n_ba,))],
+        ],
+        compiler_params=pltpu.CompilerParams(collective_id=collective_id, has_side_effects=True),
+    )(q, q.T)
+
+
 def project(tensor, factor_two, factor_three):
     rank = factor_three.shape[1]
     local_rows = tensor.shape[0]
@@ -252,21 +402,10 @@
     rank = factor_three.shape[1]
     product = project(tensor, factor_two, factor_three)
     n_core, n_y, n_ba, n_aa = lax.axis_size("core"), lax.axis_size("y"), lax.axis_size("ba"), lax.axis_size("aa")
-    n_col = n_core * n_y
     on_chip = direct_reduce_scatter(product, ("core",), (n_core,), 5)
     columns_here = direct_reduce_scatter(ring_reduce_scatter(on_chip, "y", n_y, 0), ("ba",), (n_ba,), 3)
-    gathered = direct_all_gather(columns_here, ("aa",), (n_aa,), 2)
-    depth, rows = columns_here.shape
-    per_block = n_ba // n_aa
-    out_rows = rows * n_aa // (n_ba * n_col)
-    ordered = gathered.reshape(n_aa, depth, per_block, n_col, out_rows).transpose(3, 0, 2, 4, 1)
-    terms = jnp.einsum("cpbtm,mi->cpbti", ordered, columns_here, precision=lax.Precision.HIGHEST, preferred_element_type=jnp.float32)
-    terms = terms.reshape(n_col * n_ba * out_rows, rows)
-    gram_t = direct_reduce_scatter(terms, ("y", "core"), (n_y, n_core), 1)
-    gram_t = direct_reduce_scatter(gram_t, ("ba",), (n_ba,), 4)
+    gram_t = gram_reduce(columns_here, (n_aa, n_ba, n_y, n_core), 1)
     return gram_t.T * (1.0 / (rank * rank))
-
-
 def solution(mesh):
     n_core = 2
     shape = mesh.devices.shape

time: 112 us -> 107 us (0.955)
  matrix products: 15.5 us -> 12.7 us
  Pallas kernels: 92.4 us -> 90.1 us
    pallas_call x4 -> x2, Pallas kernels: 60.7 us -> 29.9 us  [direct_reduce_scatter(): pl.pallas_call(functools.partial(direct_rs_kernel, tuple(axes), tuple(siz...]
    pallas_call x1, Pallas kernels: 7.77 us -> 36.3 us  [gram_reduce(): pl.pallas_call(functools.partial(gram_kernel, sizes), out_shape=jax.Shape...]
    dot_general x1 -> x0, matrix products: 2.79 us -> none  [body(): jnp.einsum('cpbtm,mi->cpbti', ordered, columns_here, precision=lax.Precis...]
where the time goes in v6:
time: 107 us
  Pallas kernels  90.1 us (84%)
  matrix products  12.7 us (12%)
  local copies, waits for them, and re-layouts  2.29 us (2%)
  other arithmetic  1.33 us (1%)
    pallas_call x1, Pallas kernels, gram_reduce(): pl.pallas_call(functools.partial(gram_kernel, sizes), out_shape=jax.Shape...  36.3 us
    pallas_call x2, Pallas kernels, direct_reduce_scatter(): pl.pallas_call(functools.partial(direct_rs_kernel, tuple(axes), tuple(siz...  29.9 us
    pallas_call x1, Pallas kernels, ring_reduce_scatter(): pl.pallas_call(functools.partial(ring_kernel, axis, n), out_shape=jax.Sha...  23.9 us
    dot_general x1, matrix products, project(): jnp.einsum('ijk,ks->ijs', tensor, factor_three, preferred_element_type=jn...  6.39 us
    dot_general x1, matrix products, project(): jnp.einsum('jr,ijs->sri', factor_two, partial_value, preferred_element_ty...  6.35 us

profile of v6, /device:TPU:1, one launch (start us, length us, event | category | flops | bytes accessed | tf_op | source)
XLA Modules:
  0.0 106.5 jit_solution(2188482043170103987)
XLA Ops:
  0.0 0.0 copy-start
  0.0 0.0 copy-start.1
  0.0 0.7 copy-done
  0.7 6.4 %fusion.2 = bf16[256,128,64]{1,2,0:T(8,128)(2,1)S(1)} fusion(bf16[256,128,128]{2,1,0:T(8,128)(2,1)} %param.3, bf16[128,64]{0,1:T(8,128)(2,1)S(1)} %copy-done), kind=kOutput, calls=%fused_computation.3 | convolution fusion | flops 536870912 | bytes 12599296 | tf_op jit(solution)/shard_map/ijk,ks->ijs/dot_general | solution.py:394
  7.1 0.0 copy-done.1
  7.1 6.4 %fusion = f32[256,64,64]{0,2,1:T(8,128)} fusion(bf16[256,128,64]{1,2,0:T(8,128)(2,1)S(1)} %fusion.2, bf16[128,64]{0,1:T(8,128)(2,1)S(1)} %copy-done.1), kind=kOutput, calls=%fused_computation.1 | convolution fusion | flops 268435456 | bytes 8404992 | tf_op jit(solution)/shard_map/jr,ijs->sri/dot_general | solution.py:397
  13.5 10.6 %shard_map.37 = f32[2048,256]{1,0:T(8,128)} custom-call(f32[2,2048,256]{2,1,0:T(8,128)} %bitcast.15), custom_call_target="tpu_custom_call" | custom-call | tf_op jit(solution)/shard_map/pallas_call | solution.py:162
  24.1 23.9 %shard_map.38 = f32[512,256]{1,0:T(8,128)} custom-call(f32[4,512,256]{2,1,0:T(8,128)} %bitcast.16), custom_call_target="tpu_custom_call" | custom-call | tf_op jit(solution)/shard_map/pallas_call | solution.py:63
  48.0 19.3 %shard_map.39.q_ref = f32[64,256]{1,0:T(8,128)} custom-call(f32[8,64,256]{2,1,0:T(8,128)} %bitcast.17), custom_call_target="tpu_custom_call" | custom-call | tf_op jit(solution)/shard_map/pallas_call | solution.py:162
  67.3 1.6 %copy.4 = f32[64,256]{0,1:T(8,128)} copy(f32[64,256]{1,0:T(8,128)} %shard_map.39.q_ref) | data formatting | bytes 131072 | tf_op jit(solution)/shard_map/pallas_call | solution.py:162
  68.9 36.3 %shard_map.40 = f32[16,256]{1,0:T(8,128)} custom-call(f32[64,256]{1,0:T(8,128)} %shard_map.39.q_ref, f32[256,64]{1,0:T(8,128)} %bitcast.18), custom_call_target="tpu_custom_call" | custom-call | tf_op jit(solution)/shard_map/pallas_call | solution.py:372
  105.2 1.3 %multiply_bitcast_fusion = f32[256,16]{0,1:T(8,128)} fusion(f32[16,256]{1,0:T(8,128)} %shard_map.40), kind=kLoop, calls=%fused_computation.5 | loop fusion | flops 4096 | bytes 32768 | tf_op jit(solution)/shard_map/mul | solution.py:408
Async XLA Ops:
  0.0 0.7 copy-start
  0.0 7.1 %copy-start.1 = (bf16[128,64]{0,1:T(8,128)(2,1)S(1)}, bf16[128,64]{0,1:T(8,128)(2,1)}, u32[]{:S(2)}) copy-start(bf16[128,64]{0,1:T(8,128)(2,1)} %param.4) | copy-start | bytes 49156

commit v7 on v1

v7 whole, which is shorter than its diff:
```python
import functools

import jax
import jax.numpy as jnp
from jax import lax
from jax.experimental import pallas as pl
from jax.experimental.pallas import tpu as pltpu
from jax.sharding import PartitionSpec as P

MESH = pl.DeviceIdType.MESH


def remote(src, dst, send, recv, dev):
    return pltpu.make_async_remote_copy(
        src_ref=src, dst_ref=dst, send_sem=send, recv_sem=recv, device_id=dev, device_id_type=MESH
    )


def direct_phase(n, me, dev, x_ref, out_ref, recv, send_sem, recv_sem, blk=None):
    def piece(k):
        return x_ref.at[k] if blk is None else x_ref.at[pl.ds(k * blk, blk)]

    def outgoing(peer):
        return remote(piece(peer), recv.at[me], send_sem.at[peer], recv_sem.at[me], dev(peer))

    def incoming(peer):
        return remote(piece(me), recv.at[peer], send_sem.at[peer], recv_sem.at[peer], dev(peer))

    def start(step, carry):
        outgoing(lax.rem(me + step, n)).start()
        return carry

    lax.fori_loop(1, n, start, 0)
    out_ref[...] = piece(me)[...]

    def gather(step, carry):
        peer = lax.rem(me + n - step, n)
        incoming(peer).wait_recv()
        out_ref[...] += recv[peer]
        return carry

    lax.fori_loop(1, n, gather, 0)

    def finish(step, carry):
        outgoing(lax.rem(me + step, n)).wait_send()
        return carry

    lax.fori_loop(1, n, finish, 0)


def ring_phase(n, me, dev, x_ref, out_ref, recv, sendbuf, send_sem, recv_sem):
    right = lax.rem(me + 1, n)
    left = lax.rem(me + n - 1, n)
    half = x_ref.shape[1] // 2
    lanes = (pl.ds(0, half), pl.ds(half, half))
    towards = (right, left)

    def chunk_sent(d, step):
        return lax.rem(me - step - 1 + 2 * n, n) if d == 0 else lax.rem(me + step + 1, n)

    for step in range(n - 1):
        copies = []
        for d in range(2):
            src = x_ref.at[chunk_sent(d, 0), lanes[d]] if step == 0 else sendbuf.at[d, step]
            copy = remote(src, recv.at[d, step], send_sem.at[d, step], recv_sem.at[d, step], dev(towards[d]))
            copy.start()
            copies.append(copy)
        for d in range(2):
            copies[d].wait_recv()
            total = recv[d, step] + x_ref[chunk_sent(d, step + 1), lanes[d]]
            if step < n - 2:
                sendbuf[d, step + 1] = total
            else:
                out_ref[lanes[d]] = total
        for d in range(2):
            copies[d].wait_send()


def whole_kernel(sizes, x_ref, out_ref, core_recv, on_chip, ring_recv, ring_send, ring_out, ba_recv, q_buf,
                 gath, terms, recv_col, part, recv_ba, sems):
    n_aa, n_ba, n_y, n_core = sizes
    n_col = n_y * n_core
    per_block = n_ba // n_aa
    out_rows = out_ref.shape[0]
    (s_core, r_core, s_ring, r_ring, s_ba1, r_ba1, send_g, recv_g, send_c, recv_c, send_b, recv_b) = sems
    me_aa = lax.axis_index("aa")
    me_ba = lax.axis_index("ba")
    me_y = lax.axis_index("y")
    me_core = lax.axis_index("core")
    me_col = me_y * n_core + me_core

    def aa_dev(p):
        return {"aa": p}

    def col_dev(c):
        return {"y": c // n_core, "core": lax.rem(c, n_core)}

    def ba_dev(b):
        return {"ba": b}

    def core_dev(k):
        return {"core": k}

    def y_dev(k):
        return {"y": k}

    barrier = pltpu.get_barrier_semaphore()
    groups = ((n_aa, me_aa, aa_dev), (n_col, me_col, col_dev), (n_ba, me_ba, ba_dev))
    for n, me, dev in groups:
        def greet(step, carry, n=n, me=me, dev=dev):
            pl.semaphore_signal(barrier, inc=1, device_id=dev(lax.rem(me + step, n)), device_id_type=MESH)
            return carry

        lax.fori_loop(1, n, greet, 0)
    pl.semaphore_wait(barrier, n_aa + n_col + n_ba - 3)

    direct_phase(n_core, me_core, core_dev, x_ref, on_chip, core_recv, s_core, r_core)
    ring_phase(n_y, me_y, y_dev, on_chip, ring_out, ring_recv, ring_send, s_ring, r_ring)
    direct_phase(n_ba, me_ba, ba_dev, ring_out, q_buf, ba_recv, s_ba1, r_ba1, blk=q_buf.shape[0])

    q = q_buf[...]
    gath[me_aa] = q

    def g_out(p):
        return remote(q_buf, gath.at[me_aa], send_g.at[p], recv_g.at[me_aa], aa_dev(p))

    def g_in(p):
        return remote(q_buf, gath.at[p], send_g.at[p], recv_g.at[p], aa_dev(p))

    def g_start(step, carry):
        g_out(lax.rem(me_aa + step, n_aa)).start()
        return carry

    lax.fori_loop(1, n_aa, g_start, 0)

    def g_wait(step, carry):
        g_in(lax.rem(me_aa + n_aa - step, n_aa)).wait_recv()
        return carry

    lax.fori_loop(1, n_aa, g_wait, 0)

    def g_done(step, carry):
        g_out(lax.rem(me_aa + step, n_aa)).wait_send()
        return carry

    lax.fori_loop(1, n_aa, g_done, 0)

    blocks = [gath[p].T for p in range(n_aa)]
    for c in range(n_col):
        pieces = []
        for p in range(n_aa):
            for b2 in range(per_block):
                start = b2 * n_col * out_rows + c * out_rows
                pieces.append(blocks[p][start:start + out_rows, :])
        lhs = jnp.concatenate(pieces, axis=0)
        block = jnp.dot(lhs, q, precision=lax.Precision.HIGHEST, preferred_element_type=jnp.float32)
        terms[c] = block.reshape(n_ba, out_rows, q.shape[1])

    direct_phase(n_col, me_col, col_dev, terms, part, recv_col, send_c, recv_c)
    direct_phase(n_ba, me_ba, ba_dev, part, out_ref, recv_ba, send_b, recv_b)


def reduce_and_gram(product, sizes, collective_id):
    n_aa, n_ba, n_y, n_core = sizes
    n_col = n_y * n_core
    depth_all, rows = product.shape
    depth = depth_all // (n_core * n_y * n_ba)
    out_rows = rows * n_aa // (n_ba * n_col)
    rows_c = depth_all // n_core
    rows_y = rows_c // n_y
    half = rows_y // 2
    f32 = jnp.float32
    dma = pltpu.SemaphoreType.DMA
    return pl.pallas_call(
        functools.partial(whole_kernel, sizes),
        out_shape=jax.ShapeDtypeStruct((out_rows, rows), f32),
        in_specs=[pl.BlockSpec(memory_space=pltpu.VMEM)],
        out_specs=pl.BlockSpec(memory_space=pltpu.VMEM),
        scratch_shapes=[
            pltpu.VMEM((n_core, n_y, rows_y, rows), f32),
            pltpu.VMEM((n_y, rows_y, rows), f32),
            pltpu.VMEM((2, n_y - 1, half, rows), f32),
            pltpu.VMEM((2, n_y - 1, half, rows), f32),
            pltpu.VMEM((rows_y, rows), f32),
            pltpu.VMEM((n_ba, depth, rows), f32),
            pltpu.VMEM((depth, rows), f32),
            pltpu.VMEM((n_aa, depth, rows), f32),
            pltpu.VMEM((n_col, n_ba, out_rows, rows), f32),
            pltpu.VMEM((n_col, n_ba, out_rows, rows), f32),
            pltpu.VMEM((n_ba, out_rows, rows), f32),
            pltpu.VMEM((n_ba, out_rows, rows), f32),
            [dma((n_core,)), dma((n_core,)), dma((2, n_y - 1)), dma((2, n_y - 1)), dma((n_ba,)), dma((n_ba,)),
             dma((n_aa,)), dma((n_aa,)), dma((n_col,)), dma((n_col,)), dma((n_ba,)), dma((n_ba,))],
        ],
        compiler_params=pltpu.CompilerParams(collective_id=collective_id, has_side_effects=True),
    )(product.reshape(n_core, n_y, rows_y, rows))


def project(tensor, factor_two, factor_three):
    rank = factor_three.shape[1]
    local_rows = tensor.shape[0]
    partial_value = jnp.einsum(
        "ijk,ks->ijs", tensor, factor_three, preferred_element_type=jnp.float32
    ).astype(jnp.bfloat16)
    product = jnp.einsum("jr,ijs->sri", factor_two, partial_value, preferred_element_type=jnp.float32)
    return product.reshape(rank * rank, local_rows)


def body(tensor, factor_two, factor_three):
    rank = factor_three.shape[1]
    product = project(tensor, factor_two, factor_three)
    sizes = (lax.axis_size("aa"), lax.axis_size("ba"), lax.axis_size("y"), lax.axis_size("core"))
    gram_t = reduce_and_gram(product, sizes, 0)
    return gram_t.T * (1.0 / (rank * rank))
def solution(mesh):
    n_core = 2
    shape = mesh.devices.shape
    split = jax.sharding.Mesh(
        mesh.devices.reshape(shape[0], shape[1], shape[2] // n_core, n_core), ("aa", "ba", "y", "core")
    )
    return jax.shard_map(
        body,
        mesh=split,
        in_specs=(P("aa", "ba", ("y", "core")), P("ba", None), P(("y", "core"), None)),
        out_specs=P("aa", ("ba", "y", "core")),
        check_vma=False,
    )
```

time: 152 us -> 91.9 us (0.60)
  blocking collectives: 129 us -> 0 us
  Pallas kernels: 0 us -> 76.9 us
  local copies, waits for them, and re-layouts: 8.3 us -> 0.72 us
  other arithmetic: 3.24 us -> 1.33 us
  matrix products: 11 us -> 12.7 us
    all_to_all x4 -> x0, blocking collectives: 120 us -> none  [a2a_rs(): got = lax.all_to_all(parts, axis, 0, 0, tiled=False)]
    pallas_call x0 -> x1, Pallas kernels: none -> 76.9 us  [reduce_and_gram(): pl.pallas_call(functools.partial(whole_kernel, sizes), out_shape=jax.Shap...]
    all_gather x1 -> x0, blocking collectives: 9.73 us -> none  [body(): gathered = lax.all_gather(columns_here, 'aa', axis=1, tiled=True)]
    another operation x1 -> x0, local copies, waits for them, and re-layouts: 4.87 us -> none  [a2a_rs(): parts = x.reshape(n, x.shape[0] // n, *x.shape[1:])]
    convert_element_type x1 -> x0, local copies, waits for them, and re-layouts: 2.7 us -> none  [project(): partial_value = jnp.einsum('ijk,ks->jsi', tensor, factor_three, preferred...]
    reduce_sum x4 -> x0, other arithmetic: 2.63 us -> none  [a2a_rs(): return got.sum(axis=0)]
    dot_general x3 -> x2, matrix products: 11 us -> 12.7 us  [the longest x1 6.39 us: project(): jnp.einsum('ijk,ks->ijs', tensor, factor_three, preferred_element_type=jn...]
where the time goes in v7:
time: 91.9 us; the launch traced here: 91.7 us
  Pallas kernels  76.9 us (84%)
  matrix products  12.7 us (14%)
  other arithmetic  1.33 us (1%)
    pallas_call x1, Pallas kernels, reduce_and_gram(): pl.pallas_call(functools.partial(whole_kernel, sizes), out_shape=jax.Shap...  76.9 us
    dot_general x1, matrix products, project(): jnp.einsum('ijk,ks->ijs', tensor, factor_three, preferred_element_type=jn...  6.39 us
    dot_general x1, matrix products, project(): jnp.einsum('jr,ijs->sri', factor_two, partial_value, preferred_element_ty...  6.35 us

profile of v7, /device:TPU:1, one launch (start us, length us, event | category | flops | bytes accessed | tf_op | source)
XLA Modules:
  0.0 91.7 jit_solution(3948929407661806850)
XLA Ops:
  0.0 0.0 copy-start
  0.0 0.0 copy-start.1
  0.0 0.7 copy-done
  0.7 6.4 %fusion.2 = bf16[256,128,64]{1,2,0:T(8,128)(2,1)S(1)} fusion(bf16[256,128,128]{2,1,0:T(8,128)(2,1)} %param.3, bf16[128,64]{0,1:T(8,128)(2,1)S(1)} %copy-done), kind=kOutput, calls=%fused_computation.3 | convolution fusion | flops 536870912 | bytes 12599296 | tf_op jit(solution)/shard_map/ijk,ks->ijs/dot_general | solution.py:202
  7.1 0.0 copy-done.1
  7.1 6.4 %fusion = f32[256,64,64]{0,2,1:T(8,128)} fusion(bf16[256,128,64]{1,2,0:T(8,128)(2,1)S(1)} %fusion.2, bf16[128,64]{0,1:T(8,128)(2,1)S(1)} %copy-done.1), kind=kOutput, calls=%fused_computation.1 | convolution fusion | flops 268435456 | bytes 8404992 | tf_op jit(solution)/shard_map/jr,ijs->sri/dot_general | solution.py:205
  13.5 76.9 %shard_map.37 = f32[16,256]{1,0:T(8,128)} custom-call(f32[2,4,512,256]{3,2,1,0:T(8,128)} %bitcast.12), custom_call_target="tpu_custom_call" | custom-call | tf_op jit(solution)/shard_map/pallas_call | solution.py:174
  90.3 1.3 %multiply_bitcast_fusion = f32[256,16]{0,1:T(8,128)} fusion(f32[16,256]{1,0:T(8,128)} %shard_map.37), kind=kLoop, calls=%fused_computation.5 | loop fusion | flops 4096 | bytes 32768 | tf_op jit(solution)/shard_map/mul | solution.py:214
Async XLA Ops:
  0.0 0.7 copy-start
  0.0 7.1 %copy-start.1 = (bf16[128,64]{0,1:T(8,128)(2,1)S(1)}, bf16[128,64]{0,1:T(8,128)(2,1)}, u32[]{:S(2)}) copy-start(bf16[128,64]{0,1:T(8,128)(2,1)} %param.4) | copy-start | bytes 49156

commit v8 on v7

--- a/solution.py
+++ b/solution.py
@@ -48,6 +48,64 @@
     lax.fori_loop(1, n, finish, 0)
 
 
+def direct_start(n, me, dev, x_ref, recv, send_sem, recv_sem, blk):
+    def start(step, carry):
+        peer = lax.rem(me + step, n)
+        remote(x_ref.at[pl.ds(peer * blk, blk)], recv.at[me], send_sem.at[peer], recv_sem.at[me], dev(peer)).start()
+        return carry
+
+    lax.fori_loop(1, n, start, 0)
+
+
+def direct_finish(n, me, dev, x_ref, out_ref, recv, send_sem, recv_sem, blk):
+    out_ref[...] = x_ref[pl.ds(me * blk, blk)]
+
+    def gather(step, carry):
+        peer = lax.rem(me + n - step, n)
+        remote(x_ref.at[pl.ds(me * blk, blk)], recv.at[peer], send_sem.at[peer], recv_sem.at[peer], dev(peer)).wait_recv()
+        out_ref[...] += recv[peer]
+        return carry
+
+    lax.fori_loop(1, n, gather, 0)
+
+    def finish(step, carry):
+        peer = lax.rem(me + step, n)
+        remote(x_ref.at[pl.ds(peer * blk, blk)], recv.at[me], send_sem.at[peer], recv_sem.at[me], dev(peer)).wait_send()
+        return carry
+
+    lax.fori_loop(1, n, finish, 0)
+
+
+def ring_flat(n, me, dev, x_ref, out_ref, recv, sendbuf, send_sem, recv_sem, blk):
+    right = lax.rem(me + 1, n)
+    left = lax.rem(me + n - 1, n)
+    half = blk // 2
+    towards = (right, left)
+
+    def chunk_sent(d, step):
+        return lax.rem(me - step - 1 + 2 * n, n) if d == 0 else lax.rem(me + step + 1, n)
+
+    def rows_of(d, chunk):
+        return pl.ds(chunk * blk + d * half, half)
+
+    for step in range(n - 1):
+        copies = []
+        for d in range(2):
+            src = x_ref.at[rows_of(d, chunk_sent(d, 0))] if step == 0 else sendbuf.at[d, step]
+            copy = remote(src, recv.at[d, step], send_sem.at[d, step], recv_sem.at[d, step], dev(towards[d]))
+            copy.start()
+            copies.append(copy)
+        for d in range(2):
+            copies[d].wait_recv()
+            total = recv[d, step] + x_ref[rows_of(d, chunk_sent(d, step + 1))]
+            if step < n - 2:
+                sendbuf[d, step + 1] = total
+            else:
+                out_ref[pl.ds(d * half, half)] = total
+        for d in range(2):
+            copies[d].wait_send()
+
+
 def ring_phase(n, me, dev, x_ref, out_ref, recv, sendbuf, send_sem, recv_sem):
     right = lax.rem(me + 1, n)
     left = lax.rem(me + n - 1, n)
@@ -76,13 +134,13 @@
             copies[d].wait_send()
 
 
-def whole_kernel(sizes, x_ref, out_ref, core_recv, on_chip, ring_recv, ring_send, ring_out, ba_recv, q_buf,
-                 gath, terms, recv_col, part, recv_ba, sems):
+def whole_kernel(sizes, x_ref, out_ref, core_recv, on_chip, ring_a_recv, ring_a_send, ring_a_out, z_b_recv, z_b_out,
+                 z_a_recv, ring_b_recv, ring_b_send, q_buf, gath, terms, recv_col, part, recv_ba, sems):
     n_aa, n_ba, n_y, n_core = sizes
     n_col = n_y * n_core
     per_block = n_ba // n_aa
     out_rows = out_ref.shape[0]
-    (s_core, r_core, s_ring, r_ring, s_ba1, r_ba1, send_g, recv_g, send_c, recv_c, send_b, recv_b) = sems
+    (s_core, r_core, s_ra, r_ra, s_zb, r_zb, s_za, r_za, s_rb, r_rb, send_g, recv_g, send_c, recv_c, send_b, recv_b) = sems
     me_aa = lax.axis_index("aa")
     me_ba = lax.axis_index("ba")
     me_y = lax.axis_index("y")
@@ -115,8 +173,19 @@
     pl.semaphore_wait(barrier, n_aa + n_col + n_ba - 3)
 
     direct_phase(n_core, me_core, core_dev, x_ref, on_chip, core_recv, s_core, r_core)
-    ring_phase(n_y, me_y, y_dev, on_chip, ring_out, ring_recv, ring_send, s_ring, r_ring)
-    direct_phase(n_ba, me_ba, ba_dev, ring_out, q_buf, ba_recv, s_ba1, r_ba1, blk=q_buf.shape[0])
+    rows_a = on_chip.shape[0] * 3 // 4
+    rows_b = on_chip.shape[0] - rows_a
+    part_a = on_chip.at[pl.ds(0, rows_a)]
+    part_b = on_chip.at[pl.ds(rows_a, rows_b)]
+    blk_zb = rows_b // n_ba
+    direct_start(n_ba, me_ba, ba_dev, part_b, z_b_recv, s_zb, r_zb, blk_zb)
+    ring_flat(n_y, me_y, y_dev, part_a, ring_a_out, ring_a_recv, ring_a_send, s_ra, r_ra, rows_a // n_y)
+    direct_finish(n_ba, me_ba, ba_dev, part_b, z_b_out, z_b_recv, s_zb, r_zb, blk_zb)
+    depth_a = ring_a_out.shape[0] // n_ba
+    depth_b = blk_zb // n_y
+    direct_start(n_ba, me_ba, ba_dev, ring_a_out, z_a_recv, s_za, r_za, depth_a)
+    ring_flat(n_y, me_y, y_dev, z_b_out, q_buf.at[pl.ds(depth_a, depth_b)], ring_b_recv, ring_b_send, s_rb, r_rb, depth_b)
+    direct_finish(n_ba, me_ba, ba_dev, ring_a_out, q_buf.at[pl.ds(0, depth_a)], z_a_recv, s_za, r_za, depth_a)
 
     q = q_buf[...]
     gath[me_aa] = q
@@ -167,8 +236,11 @@
     depth = depth_all // (n_core * n_y * n_ba)
     out_rows = rows * n_aa // (n_ba * n_col)
     rows_c = depth_all // n_core
-    rows_y = rows_c // n_y
-    half = rows_y // 2
+    rows_a = rows_c * 3 // 4
+    blk_a = rows_a // n_y
+    blk_zb = (rows_c - rows_a) // n_ba
+    depth_a = blk_a // n_ba
+    depth_b = blk_zb // n_y
     f32 = jnp.float32
     dma = pltpu.SemaphoreType.DMA
     return pl.pallas_call(
@@ -177,12 +249,16 @@
         in_specs=[pl.BlockSpec(memory_space=pltpu.VMEM)],
         out_specs=pl.BlockSpec(memory_space=pltpu.VMEM),
         scratch_shapes=[
-            pltpu.VMEM((n_core, n_y, rows_y, rows), f32),
-            pltpu.VMEM((n_y, rows_y, rows), f32),
-            pltpu.VMEM((2, n_y - 1, half, rows), f32),
-            pltpu.VMEM((2, n_y - 1, half, rows), f32),
-            pltpu.VMEM((rows_y, rows), f32),
-            pltpu.VMEM((n_ba, depth, rows), f32),
+            pltpu.VMEM((n_core, rows_c, rows), f32),
+            pltpu.VMEM((rows_c, rows), f32),
+            pltpu.VMEM((2, n_y - 1, blk_a // 2, rows), f32),
+            pltpu.VMEM((2, n_y - 1, blk_a // 2, rows), f32),
+            pltpu.VMEM((blk_a, rows), f32),
+            pltpu.VMEM((n_ba, blk_zb, rows), f32),
+            pltpu.VMEM((blk_zb, rows), f32),
+            pltpu.VMEM((n_ba, depth_a, rows), f32),
+            pltpu.VMEM((2, n_y - 1, depth_b // 2, rows), f32),
+            pltpu.VMEM((2, n_y - 1, depth_b // 2, rows), f32),
             pltpu.VMEM((depth, rows), f32),
             pltpu.VMEM((n_aa, depth, rows), f32),
             pltpu.VMEM((n_col, n_ba, out_rows, rows), f32),
@@ -190,10 +266,11 @@
             pltpu.VMEM((n_ba, out_rows, rows), f32),
             pltpu.VMEM((n_ba, out_rows, rows), f32),
             [dma((n_core,)), dma((n_core,)), dma((2, n_y - 1)), dma((2, n_y - 1)), dma((n_ba,)), dma((n_ba,)),
+             dma((n_ba,)), dma((n_ba,)), dma((2, n_y - 1)), dma((2, n_y - 1)),
              dma((n_aa,)), dma((n_aa,)), dma((n_col,)), dma((n_col,)), dma((n_ba,)), dma((n_ba,))],
         ],
         compiler_params=pltpu.CompilerParams(collective_id=collective_id, has_side_effects=True),
-    )(product.reshape(n_core, n_y, rows_y, rows))
+    )(product.reshape(n_core, rows_c, rows))
 
 
 def project(tensor, factor_two, factor_three):

time: 91.9 us -> 86.1 us (0.937)
  Pallas kernels: 76.9 us -> 71 us
    pallas_call x1, Pallas kernels: 76.9 us -> 71 us  [reduce_and_gram(): pl.pallas_call(functools.partial(whole_kernel, sizes), out_shape=jax.Shap...]
where the time goes in v8:
time: 86.1 us; the launch traced here: 85.8 us
  Pallas kernels  71 us (82%)
  matrix products  12.7 us (15%)
  other arithmetic  1.33 us (2%)
    pallas_call x1, Pallas kernels, reduce_and_gram(): pl.pallas_call(functools.partial(whole_kernel, sizes), out_shape=jax.Shap...  71 us
    dot_general x1, matrix products, project(): jnp.einsum('ijk,ks->ijs', tensor, factor_three, preferred_element_type=jn...  6.39 us
    dot_general x1, matrix products, project(): jnp.einsum('jr,ijs->sri', factor_two, partial_value, preferred_element_ty...  6.35 us

profile of v8, /device:TPU:1, one launch (start us, length us, event | category | flops | bytes accessed | tf_op | source)
XLA Modules:
  0.0 85.8 jit_solution(10007701541586387489)
XLA Ops:
  0.0 0.0 copy-start
  0.0 0.0 copy-start.1
  0.0 0.7 copy-done
  0.7 6.4 %fusion.2 = bf16[256,128,64]{1,2,0:T(8,128)(2,1)S(1)} fusion(bf16[256,128,128]{2,1,0:T(8,128)(2,1)} %param.3, bf16[128,64]{0,1:T(8,128)(2,1)S(1)} %copy-done), kind=kOutput, calls=%fused_computation.3 | convolution fusion | flops 536870912 | bytes 12599296 | tf_op jit(solution)/shard_map/ijk,ks->ijs/dot_general | solution.py:279
  7.1 0.0 copy-done.1
  7.1 6.4 %fusion = f32[256,64,64]{0,2,1:T(8,128)} fusion(bf16[256,128,64]{1,2,0:T(8,128)(2,1)S(1)} %fusion.2, bf16[128,64]{0,1:T(8,128)(2,1)S(1)} %copy-done.1), kind=kOutput, calls=%fused_computation.1 | convolution fusion | flops 268435456 | bytes 8404992 | tf_op jit(solution)/shard_map/jr,ijs->sri/dot_general | solution.py:282
  13.5 71.0 %shard_map.37 = f32[16,256]{1,0:T(8,128)} custom-call(f32[2,2048,256]{2,1,0:T(8,128)} %bitcast.12), custom_call_target="tpu_custom_call" | custom-call | tf_op jit(solution)/shard_map/pallas_call | solution.py:246
  84.5 1.3 %multiply_bitcast_fusion = f32[256,16]{0,1:T(8,128)} fusion(f32[16,256]{1,0:T(8,128)} %shard_map.37), kind=kLoop, calls=%fused_computation.5 | loop fusion | flops 4096 | bytes 32768 | tf_op jit(solution)/shard_map/mul | solution.py:291
Async XLA Ops:
  0.0 0.7 copy-start
  0.0 7.1 %copy-start.1 = (bf16[128,64]{0,1:T(8,128)(2,1)S(1)}, bf16[128,64]{0,1:T(8,128)(2,1)}, u32[]{:S(2)}) copy-start(bf16[128,64]{0,1:T(8,128)(2,1)} %param.4) | copy-start | bytes 49156

commit v9 on v8

--- a/solution.py
+++ b/solution.py
@@ -135,7 +135,7 @@
 
 
 def whole_kernel(sizes, x_ref, out_ref, core_recv, on_chip, ring_a_recv, ring_a_send, ring_a_out, z_b_recv, z_b_out,
-                 z_a_recv, ring_b_recv, ring_b_send, q_buf, gath, terms, recv_col, part, recv_ba, sems):
+                 z_a_recv, ring_b_recv, ring_b_send, q_buf, gath, gt, terms, recv_col, part, recv_ba, sems):
     n_aa, n_ba, n_y, n_core = sizes
     n_col = n_y * n_core
     per_block = n_ba // n_aa
@@ -214,18 +214,47 @@
 
     lax.fori_loop(1, n_aa, g_done, 0)
 
-    blocks = [gath[p].T for p in range(n_aa)]
-    for c in range(n_col):
+    for p in range(n_aa):
+        gt[p] = gath[p].T
+
+    def term_block(c):
         pieces = []
         for p in range(n_aa):
             for b2 in range(per_block):
-                start = b2 * n_col * out_rows + c * out_rows
-                pieces.append(blocks[p][start:start + out_rows, :])
+                start = pl.multiple_of(b2 * n_col * out_rows + c * out_rows, out_rows)
+                pieces.append(gt[p, pl.ds(start, out_rows), :])
         lhs = jnp.concatenate(pieces, axis=0)
         block = jnp.dot(lhs, q, precision=lax.Precision.HIGHEST, preferred_element_type=jnp.float32)
-        terms[c] = block.reshape(n_ba, out_rows, q.shape[1])
-
-    direct_phase(n_col, me_col, col_dev, terms, part, recv_col, send_c, recv_c)
+        return block.reshape(n_ba, out_rows, q.shape[1])
+
+    def c_out(c):
+        return remote(terms.at[c], recv_col.at[me_col], send_c.at[c], recv_c.at[me_col], col_dev(c))
+
+    def c_in(c):
+        return remote(terms.at[me_col], recv_col.at[c], send_c.at[c], recv_c.at[c], col_dev(c))
+
+    def c_start(step, carry):
+        c = lax.rem(me_col + step, n_col)
+        terms[c] = term_block(c)
+        c_out(c).start()
+        return carry
+
+    lax.fori_loop(1, n_col, c_start, 0)
+    part[...] = term_block(me_col)
+
+    def c_wait(step, carry):
+        peer = lax.rem(me_col + n_col - step, n_col)
+        c_in(peer).wait_recv()
+        part[...] += recv_col[peer]
+        return carry
+
+    lax.fori_loop(1, n_col, c_wait, 0)
+
+    def c_done(step, carry):
+        c_out(lax.rem(me_col + step, n_col)).wait_send()
+        return carry
+
+    lax.fori_loop(1, n_col, c_done, 0)
     direct_phase(n_ba, me_ba, ba_dev, part, out_ref, recv_ba, send_b, recv_b)
 
 
@@ -261,6 +290,7 @@
             pltpu.VMEM((2, n_y - 1, depth_b // 2, rows), f32),
             pltpu.VMEM((depth, rows), f32),
             pltpu.VMEM((n_aa, depth, rows), f32),
+            pltpu.VMEM((n_aa, rows, depth), f32),
             pltpu.VMEM((n_col, n_ba, out_rows, rows), f32),
             pltpu.VMEM((n_col, n_ba, out_rows, rows), f32),
             pltpu.VMEM((n_ba, out_rows, rows), f32),
@@ -276,9 +306,10 @@
 def project(tensor, factor_two, factor_three):
     rank = factor_three.shape[1]
     local_rows = tensor.shape[0]
-    partial_value = jnp.einsum(
-        "ijk,ks->ijs", tensor, factor_three, preferred_element_type=jnp.float32
-    ).astype(jnp.bfloat16)
+    local_two = tensor.shape[1]
+    partial_value = jnp.dot(
+        tensor.reshape(local_rows * local_two, tensor.shape[2]), factor_three, preferred_element_type=jnp.float32
+    ).astype(jnp.bfloat16).reshape(local_rows, local_two, rank)
     product = jnp.einsum("jr,ijs->sri", factor_two, partial_value, preferred_element_type=jnp.float32)
     return product.reshape(rank * rank, local_rows)
 

time: 86.1 us -> 83.8 us (0.973)
  matrix products: 12.7 us -> 9.9 us
  local copies, waits for them, and re-layouts: 0.72 us -> 1.88 us
    dot_general x1, matrix products: 6.35 us -> 3.5 us  [project(): jnp.einsum('jr,ijs->sri', factor_two, partial_value, preferred_element_ty...]
    unnamed x4 -> x5, local copies, waits for them, and re-layouts: 0.72 us -> 1.88 us
where the time goes in v9:
time: 83.8 us; the launch traced here: 83.5 us
  Pallas kernels  70.3 us (84%)
  matrix products  9.9 us (12%)
  local copies, waits for them, and re-layouts  1.88 us (2%)
  other arithmetic  1.33 us (2%)
    pallas_call x1, Pallas kernels, reduce_and_gram(): pl.pallas_call(functools.partial(whole_kernel, sizes), out_shape=jax.Shap...  70.3 us
    dot_general x1, matrix products, project(): jnp.dot(tensor.reshape(local_rows * local_two, tensor.shape[2]), factor_t...  6.39 us
    dot_general x1, matrix products, project(): jnp.einsum('jr,ijs->sri', factor_two, partial_value, preferred_element_ty...  3.5 us
    unnamed x5, local copies, waits for them, and re-layouts  1.88 us

profile of v9, /device:TPU:1, one launch (start us, length us, event | category | flops | bytes accessed | tf_op | source)
XLA Modules:
  0.0 83.5 jit_solution(4124420626238105475)
XLA Ops:
  0.0 0.0 copy-start
  0.0 0.7 copy-done
  0.7 6.4 %fusion = bf16[8,8,256,128]{3,1,2,0:T(8,128)(2,1)S(1)} fusion(bf16[32768,128]{1,0:T(8,128)(2,1)} %bitcast.19, bf16[128,64]{0,1:T(8,128)(2,1)S(1)} %copy-done), kind=kOutput, calls=%fused_computation.1 | convolution fusion | flops 538968064 | bytes 12599296 | tf_op jit(solution)/shard_map/dot_general | solution.py:310
  7.1 0.0 copy-start.1
  7.1 1.2 %copy.4 = bf16[8,8,256,128]{3,2,1,0:T(8,128)(2,1)S(1)} copy(bf16[8,8,256,128]{3,1,2,0:T(8,128)(2,1)S(1)} %fusion) | data formatting | bytes 8388608
  8.3 0.0 copy-done.1
  8.3 3.5 %fusion.1 = f32[256,64,64]{0,2,1:T(8,128)} fusion(bf16[256,128,64]{1,0,2:T(8,128)(2,1)S(1)} %bitcast.17, bf16[128,64]{0,1:T(8,128)(2,1)S(1)} %copy-done.1), kind=kOutput, calls=%fused_computation.2 | convolution fusion | flops 268435456 | bytes 8404992 | tf_op jit(solution)/shard_map/jr,ijs->sri/dot_general | solution.py:313
  11.8 70.3 %shard_map.37 = f32[16,256]{1,0:T(8,128)} custom-call(f32[2,2048,256]{2,1,0:T(8,128)} %bitcast.18), custom_call_target="tpu_custom_call" | custom-call | tf_op jit(solution)/shard_map/pallas_call | solution.py:275
  82.2 1.3 %multiply_bitcast_fusion = f32[256,16]{0,1:T(8,128)} fusion(f32[16,256]{1,0:T(8,128)} %shard_map.37), kind=kLoop, calls=%fused_computation.4 | loop fusion | flops 4096 | bytes 32768 | tf_op jit(solution)/shard_map/mul | solution.py:322
Async XLA Ops:
  0.0 0.7 copy-start
  7.1 1.2 %copy-start.1 = (bf16[128,64]{0,1:T(8,128)(2,1)S(1)}, bf16[128,64]{0,1:T(8,128)(2,1)}, u32[]{:S(2)}) copy-start(bf16[128,64]{0,1:T(8,128)(2,1)} %param.4) | copy-start | bytes 49156

commit v10 on v9

--- a/solution.py
+++ b/solution.py
@@ -172,13 +172,48 @@
         lax.fori_loop(1, n, greet, 0)
     pl.semaphore_wait(barrier, n_aa + n_col + n_ba - 3)
 
-    direct_phase(n_core, me_core, core_dev, x_ref, on_chip, core_recv, s_core, r_core)
     rows_a = on_chip.shape[0] * 3 // 4
     rows_b = on_chip.shape[0] - rows_a
-    part_a = on_chip.at[pl.ds(0, rows_a)]
-    part_b = on_chip.at[pl.ds(rows_a, rows_b)]
+    spans = (pl.ds(0, rows_a), pl.ds(rows_a, rows_b))
+
+    def core_copy(k, src, dst, peer):
+        return remote(x_ref.at[src, spans[k]], core_recv.at[dst, spans[k]], s_core.at[k, peer], r_core.at[k, dst],
+                      core_dev(peer))
+
+    def core_start(k):
+        def start(step, carry):
+            peer = lax.rem(me_core + step, n_core)
+            core_copy(k, peer, me_core, peer).start()
+            return carry
+
+        lax.fori_loop(1, n_core, start, 0)
+
+    def core_finish(k):
+        on_chip[spans[k]] = x_ref[me_core, spans[k]]
+
+        def gather(step, carry):
+            peer = lax.rem(me_core + n_core - step, n_core)
+            core_copy(k, me_core, peer, peer).wait_recv()
+            on_chip[spans[k]] += core_recv[peer, spans[k]]
+            return carry
+
+        lax.fori_loop(1, n_core, gather, 0)
+
+        def finish(step, carry):
+            peer = lax.rem(me_core + step, n_core)
+            core_copy(k, peer, me_core, peer).wait_send()
+            return carry
+
+        lax.fori_loop(1, n_core, finish, 0)
+
+    core_start(1)
+    core_start(0)
+    core_finish(1)
+    part_a = on_chip.at[spans[0]]
+    part_b = on_chip.at[spans[1]]
     blk_zb = rows_b // n_ba
     direct_start(n_ba, me_ba, ba_dev, part_b, z_b_recv, s_zb, r_zb, blk_zb)
+    core_finish(0)
     ring_flat(n_y, me_y, y_dev, part_a, ring_a_out, ring_a_recv, ring_a_send, s_ra, r_ra, rows_a // n_y)
     direct_finish(n_ba, me_ba, ba_dev, part_b, z_b_out, z_b_recv, s_zb, r_zb, blk_zb)
     depth_a = ring_a_out.shape[0] // n_ba
@@ -295,7 +330,7 @@
             pltpu.VMEM((n_col, n_ba, out_rows, rows), f32),
             pltpu.VMEM((n_ba, out_rows, rows), f32),
             pltpu.VMEM((n_ba, out_rows, rows), f32),
-            [dma((n_core,)), dma((n_core,)), dma((2, n_y - 1)), dma((2, n_y - 1)), dma((n_ba,)), dma((n_ba,)),
+            [dma((2, n_core)), dma((2, n_core)), dma((2, n_y - 1)), dma((2, n_y - 1)), dma((n_ba,)), dma((n_ba,)),
              dma((n_ba,)), dma((n_ba,)), dma((2, n_y - 1)), dma((2, n_y - 1)),
              dma((n_aa,)), dma((n_aa,)), dma((n_col,)), dma((n_col,)), dma((n_ba,)), dma((n_ba,))],
         ],

time: 83.8 us -> 82.6 us (0.986)
  Pallas kernels: 70.3 us -> 69.2 us
    pallas_call x1, Pallas kernels: 70.3 us -> 69.2 us  [reduce_and_gram(): pl.pallas_call(functools.partial(whole_kernel, sizes), out_shape=jax.Shap...]
where the time goes in v10:
time: 82.6 us; the launch traced here: 82.4 us
  Pallas kernels  69.2 us (84%)
  matrix products  9.9 us (12%)
  local copies, waits for them, and re-layouts  1.88 us (2%)
  other arithmetic  1.33 us (2%)
    pallas_call x1, Pallas kernels, reduce_and_gram(): pl.pallas_call(functools.partial(whole_kernel, sizes), out_shape=jax.Shap...  69.2 us
    dot_general x1, matrix products, project(): jnp.dot(tensor.reshape(local_rows * local_two, tensor.shape[2]), factor_t...  6.39 us
    dot_general x1, matrix products, project(): jnp.einsum('jr,ijs->sri', factor_two, partial_value, preferred_element_ty...  3.5 us
    unnamed x5, local copies, waits for them, and re-layouts  1.88 us

profile of v10, /device:TPU:1, one launch (start us, length us, event | category | flops | bytes accessed | tf_op | source)
XLA Modules:
  0.0 82.4 jit_solution(6101085419987745786)
XLA Ops:
  0.0 0.0 copy-start
  0.0 0.7 copy-done
  0.7 6.4 %fusion = bf16[8,8,256,128]{3,1,2,0:T(8,128)(2,1)S(1)} fusion(bf16[32768,128]{1,0:T(8,128)(2,1)} %bitcast.19, bf16[128,64]{0,1:T(8,128)(2,1)S(1)} %copy-done), kind=kOutput, calls=%fused_computation.1 | convolution fusion | flops 538968064 | bytes 12599296 | tf_op jit(solution)/shard_map/dot_general | solution.py:345
  7.1 0.0 copy-start.1
  7.1 1.2 %copy.4 = bf16[8,8,256,128]{3,2,1,0:T(8,128)(2,1)S(1)} copy(bf16[8,8,256,128]{3,1,2,0:T(8,128)(2,1)S(1)} %fusion) | data formatting | bytes 8388608
  8.3 0.0 copy-done.1
  8.3 3.5 %fusion.1 = f32[256,64,64]{0,2,1:T(8,128)} fusion(bf16[256,128,64]{1,0,2:T(8,128)(2,1)S(1)} %bitcast.17, bf16[128,64]{0,1:T(8,128)(2,1)S(1)} %copy-done.1), kind=kOutput, calls=%fused_computation.2 | convolution fusion | flops 268435456 | bytes 8404992 | tf_op jit(solution)/shard_map/jr,ijs->sri/dot_general | solution.py:348
  11.8 69.2 %shard_map.37 = f32[16,256]{1,0:T(8,128)} custom-call(f32[2,2048,256]{2,1,0:T(8,128)} %bitcast.18), custom_call_target="tpu_custom_call" | custom-call | tf_op jit(solution)/shard_map/pallas_call | solution.py:310
  81.0 1.3 %multiply_bitcast_fusion = f32[256,16]{0,1:T(8,128)} fusion(f32[16,256]{1,0:T(8,128)} %shard_map.37), kind=kLoop, calls=%fused_computation.4 | loop fusion | flops 4096 | bytes 32768 | tf_op jit(solution)/shard_map/mul | solution.py:357
Async XLA Ops:
  0.0 0.7 copy-start
  7.1 1.2 %copy-start.1 = (bf16[128,64]{0,1:T(8,128)(2,1)S(1)}, bf16[128,64]{0,1:T(8,128)(2,1)}, u32[]{:S(2)}) copy-start(bf16[128,64]{0,1:T(8,128)(2,1)} %param.4) | copy-start | bytes 49156

commit v11 on v10

--- a/solution.py
+++ b/solution.py
@@ -77,33 +77,34 @@
 
 
 def ring_flat(n, me, dev, x_ref, out_ref, recv, sendbuf, send_sem, recv_sem, blk):
-    right = lax.rem(me + 1, n)
-    left = lax.rem(me + n - 1, n)
-    half = blk // 2
-    towards = (right, left)
+    lanes = recv.shape[0]
+    part = blk // lanes
+    towards = (lax.rem(me + 1, n), lax.rem(me + n - 1, n))
 
     def chunk_sent(d, step):
-        return lax.rem(me - step - 1 + 2 * n, n) if d == 0 else lax.rem(me + step + 1, n)
+        return lax.rem(me - step - 1 + 2 * n, n) if d % 2 == 0 else lax.rem(me + step + 1, n)
 
     def rows_of(d, chunk):
-        return pl.ds(chunk * blk + d * half, half)
-
+        return pl.ds(chunk * blk + d * part, part)
+
+    def copy(d, step):
+        src = x_ref.at[rows_of(d, chunk_sent(d, 0))] if step == 0 else sendbuf.at[d, step]
+        return remote(src, recv.at[d, step], send_sem.at[d, step], recv_sem.at[d, step], dev(towards[d % 2]))
+
+    for d in range(lanes):
+        copy(d, 0).start()
     for step in range(n - 1):
-        copies = []
-        for d in range(2):
-            src = x_ref.at[rows_of(d, chunk_sent(d, 0))] if step == 0 else sendbuf.at[d, step]
-            copy = remote(src, recv.at[d, step], send_sem.at[d, step], recv_sem.at[d, step], dev(towards[d]))
-            copy.start()
-            copies.append(copy)
-        for d in range(2):
-            copies[d].wait_recv()
+        for d in range(lanes):
+            copy(d, step).wait_recv()
             total = recv[d, step] + x_ref[rows_of(d, chunk_sent(d, step + 1))]
             if step < n - 2:
                 sendbuf[d, step + 1] = total
+                copy(d, step + 1).start()
             else:
-                out_ref[pl.ds(d * half, half)] = total
-        for d in range(2):
-            copies[d].wait_send()
+                out_ref[pl.ds(d * part, part)] = total
+    for step in range(n - 1):
+        for d in range(lanes):
+            copy(d, step).wait_send()
 
 
 def ring_phase(n, me, dev, x_ref, out_ref, recv, sendbuf, send_sem, recv_sem):
@@ -315,8 +316,8 @@
         scratch_shapes=[
             pltpu.VMEM((n_core, rows_c, rows), f32),
             pltpu.VMEM((rows_c, rows), f32),
-            pltpu.VMEM((2, n_y - 1, blk_a // 2, rows), f32),
-            pltpu.VMEM((2, n_y - 1, blk_a // 2, rows), f32),
+            pltpu.VMEM((4, n_y - 1, blk_a // 4, rows), f32),
+            pltpu.VMEM((4, n_y - 1, blk_a // 4, rows), f32),
             pltpu.VMEM((blk_a, rows), f32),
             pltpu.VMEM((n_ba, blk_zb, rows), f32),
             pltpu.VMEM((blk_zb, rows), f32),
@@ -330,7 +331,7 @@
             pltpu.VMEM((n_col, n_ba, out_rows, rows), f32),
             pltpu.VMEM((n_ba, out_rows, rows), f32),
             pltpu.VMEM((n_ba, out_rows, rows), f32),
-            [dma((2, n_core)), dma((2, n_core)), dma((2, n_y - 1)), dma((2, n_y - 1)), dma((n_ba,)), dma((n_ba,)),
+            [dma((2, n_core)), dma((2, n_core)), dma((4, n_y - 1)), dma((4, n_y - 1)), dma((n_ba,)), dma((n_ba,)),
              dma((n_ba,)), dma((n_ba,)), dma((2, n_y - 1)), dma((2, n_y - 1)),
              dma((n_aa,)), dma((n_aa,)), dma((n_col,)), dma((n_col,)), dma((n_ba,)), dma((n_ba,))],
         ],

time: 82.6 us -> 81 us (0.981)
  Pallas kernels: 69.2 us -> 67.6 us
    pallas_call x1, Pallas kernels: 69.2 us -> 67.6 us  [reduce_and_gram(): pl.pallas_call(functools.partial(whole_kernel, sizes), out_shape=jax.Shap...]
where the time goes in v11:
time: 81 us; the launch traced here: 80.8 us
  Pallas kernels  67.6 us (83%)
  matrix products  9.9 us (12%)
  local copies, waits for them, and re-layouts  1.88 us (2%)
  other arithmetic  1.33 us (2%)
    pallas_call x1, Pallas kernels, reduce_and_gram(): pl.pallas_call(functools.partial(whole_kernel, sizes), out_shape=jax.Shap...  67.6 us
    dot_general x1, matrix products, project(): jnp.dot(tensor.reshape(local_rows * local_two, tensor.shape[2]), factor_t...  6.39 us
    dot_general x1, matrix products, project(): jnp.einsum('jr,ijs->sri', factor_two, partial_value, preferred_element_ty...  3.5 us
    unnamed x5, local copies, waits for them, and re-layouts  1.88 us

profile of v11, /device:TPU:1, one launch (start us, length us, event | category | flops | bytes accessed | tf_op | source)
XLA Modules:
  0.0 80.8 jit_solution(623351993290288880)
XLA Ops:
  0.0 0.0 copy-start
  0.0 0.7 copy-done
  0.7 6.4 %fusion = bf16[8,8,256,128]{3,1,2,0:T(8,128)(2,1)S(1)} fusion(bf16[32768,128]{1,0:T(8,128)(2,1)} %bitcast.19, bf16[128,64]{0,1:T(8,128)(2,1)S(1)} %copy-done), kind=kOutput, calls=%fused_computation.1 | convolution fusion | flops 538968064 | bytes 12599296 | tf_op jit(solution)/shard_map/dot_general | solution.py:346
  7.1 0.0 copy-start.1
  7.1 1.2 %copy.4 = bf16[8,8,256,128]{3,2,1,0:T(8,128)(2,1)S(1)} copy(bf16[8,8,256,128]{3,1,2,0:T(8,128)(2,1)S(1)} %fusion) | data formatting | bytes 8388608
  8.3 0.0 copy-done.1
  8.3 3.5 %fusion.1 = f32[256,64,64]{0,2,1:T(8,128)} fusion(bf16[256,128,64]{1,0,2:T(8,128)(2,1)S(1)} %bitcast.17, bf16[128,64]{0,1:T(8,128)(2,1)S(1)} %copy-done.1), kind=kOutput, calls=%fused_computation.2 | convolution fusion | flops 268435456 | bytes 8404992 | tf_op jit(solution)/shard_map/jr,ijs->sri/dot_general | solution.py:349
  11.8 67.6 %shard_map.37 = f32[16,256]{1,0:T(8,128)} custom-call(f32[2,2048,256]{2,1,0:T(8,128)} %bitcast.18), custom_call_target="tpu_custom_call" | custom-call | tf_op jit(solution)/shard_map/pallas_call | solution.py:311
  79.4 1.3 %multiply_bitcast_fusion = f32[256,16]{0,1:T(8,128)} fusion(f32[16,256]{1,0:T(8,128)} %shard_map.37), kind=kLoop, calls=%fused_computation.4 | loop fusion | flops 4096 | bytes 32768 | tf_op jit(solution)/shard_map/mul | solution.py:358
Async XLA Ops:
  0.0 0.7 copy-start
  7.1 1.2 %copy-start.1 = (bf16[128,64]{0,1:T(8,128)(2,1)S(1)}, bf16[128,64]{0,1:T(8,128)(2,1)}, u32[]{:S(2)}) copy-start(bf16[128,64]{0,1:T(8,128)(2,1)} %param.4) | copy-start | bytes 49156

commit v12 on v11

--- a/solution.py
+++ b/solution.py
@@ -76,7 +76,7 @@
     lax.fori_loop(1, n, finish, 0)
 
 
-def ring_flat(n, me, dev, x_ref, out_ref, recv, sendbuf, send_sem, recv_sem, blk):
+def ring_flat(n, me, dev, x_ref, out_ref, recv, sendbuf, send_sem, recv_sem, blk, ready=None):
     lanes = recv.shape[0]
     part = blk // lanes
     towards = (lax.rem(me + 1, n), lax.rem(me + n - 1, n))
@@ -93,6 +93,8 @@
 
     for d in range(lanes):
         copy(d, 0).start()
+    if ready is not None:
+        ready()
     for step in range(n - 1):
         for d in range(lanes):
             copy(d, step).wait_recv()
@@ -175,7 +177,10 @@
 
     rows_a = on_chip.shape[0] * 3 // 4
     rows_b = on_chip.shape[0] - rows_a
-    spans = (pl.ds(0, rows_a), pl.ds(rows_a, rows_b))
+    blk_a = rows_a // n_y
+    firsts = sorted({(n_y - 1) % n_y, 1 % n_y})
+    offsets = firsts + [o for o in range(n_y) if o not in firsts]
+    spans = [pl.ds(lax.rem(me_y + o, n_y) * blk_a, blk_a) for o in offsets] + [pl.ds(rows_a, rows_b)]
 
     def core_copy(k, src, dst, peer):
         return remote(x_ref.at[src, spans[k]], core_recv.at[dst, spans[k]], s_core.at[k, peer], r_core.at[k, dst],
@@ -207,15 +212,21 @@
 
         lax.fori_loop(1, n_core, finish, 0)
 
-    core_start(1)
-    core_start(0)
-    core_finish(1)
-    part_a = on_chip.at[spans[0]]
-    part_b = on_chip.at[spans[1]]
+    for k in [n_y] + list(range(n_y)):
+        core_start(k)
+    core_finish(n_y)
+    part_a = on_chip.at[pl.ds(0, rows_a)]
+    part_b = on_chip.at[pl.ds(rows_a, rows_b)]
     blk_zb = rows_b // n_ba
     direct_start(n_ba, me_ba, ba_dev, part_b, z_b_recv, s_zb, r_zb, blk_zb)
-    core_finish(0)
-    ring_flat(n_y, me_y, y_dev, part_a, ring_a_out, ring_a_recv, ring_a_send, s_ra, r_ra, rows_a // n_y)
+    for k in range(len(firsts)):
+        core_finish(k)
+
+    def rest_ready():
+        for k in range(len(firsts), n_y):
+            core_finish(k)
+
+    ring_flat(n_y, me_y, y_dev, part_a, ring_a_out, ring_a_recv, ring_a_send, s_ra, r_ra, blk_a, ready=rest_ready)
     direct_finish(n_ba, me_ba, ba_dev, part_b, z_b_out, z_b_recv, s_zb, r_zb, blk_zb)
     depth_a = ring_a_out.shape[0] // n_ba
     depth_b = blk_zb // n_y
@@ -331,7 +342,7 @@
             pltpu.VMEM((n_col, n_ba, out_rows, rows), f32),
             pltpu.VMEM((n_ba, out_rows, rows), f32),
             pltpu.VMEM((n_ba, out_rows, rows), f32),
-            [dma((2, n_core)), dma((2, n_core)), dma((4, n_y - 1)), dma((4, n_y - 1)), dma((n_ba,)), dma((n_ba,)),
+            [dma((n_y + 1, n_core)), dma((n_y + 1, n_core)), dma((4, n_y - 1)), dma((4, n_y - 1)), dma((n_ba,)), dma((n_ba,)),
              dma((n_ba,)), dma((n_ba,)), dma((2, n_y - 1)), dma((2, n_y - 1)),
              dma((n_aa,)), dma((n_aa,)), dma((n_col,)), dma((n_col,)), dma((n_ba,)), dma((n_ba,))],
         ],

time: 81 us -> 79.1 us (0.977)
  Pallas kernels: 67.6 us -> 65.7 us
    pallas_call x1, Pallas kernels: 67.6 us -> 65.7 us  [reduce_and_gram(): pl.pallas_call(functools.partial(whole_kernel, sizes), out_shape=jax.Shap...]
where the time goes in v12:
time: 79.1 us; the launch traced here: 78.9 us
  Pallas kernels  65.7 us (83%)
  matrix products  9.9 us (13%)
  local copies, waits for them, and re-layouts  1.88 us (2%)
  other arithmetic  1.33 us (2%)
    pallas_call x1, Pallas kernels, reduce_and_gram(): pl.pallas_call(functools.partial(whole_kernel, sizes), out_shape=jax.Shap...  65.7 us
    dot_general x1, matrix products, project(): jnp.dot(tensor.reshape(local_rows * local_two, tensor.shape[2]), factor_t...  6.39 us
    dot_general x1, matrix products, project(): jnp.einsum('jr,ijs->sri', factor_two, partial_value, preferred_element_ty...  3.5 us
    unnamed x5, local copies, waits for them, and re-layouts  1.88 us

profile of v12, /device:TPU:1, one launch (start us, length us, event | category | flops | bytes accessed | tf_op | source)
XLA Modules:
  0.0 78.9 jit_solution(4265732658297734466)
XLA Ops:
  0.0 0.0 copy-start
  0.0 0.7 copy-done
  0.7 6.4 %fusion = bf16[8,8,256,128]{3,1,2,0:T(8,128)(2,1)S(1)} fusion(bf16[32768,128]{1,0:T(8,128)(2,1)} %bitcast.19, bf16[128,64]{0,1:T(8,128)(2,1)S(1)} %copy-done), kind=kOutput, calls=%fused_computation.1 | convolution fusion | flops 538968064 | bytes 12599296 | tf_op jit(solution)/shard_map/dot_general | solution.py:357
  7.1 0.0 copy-start.1
  7.1 1.2 %copy.4 = bf16[8,8,256,128]{3,2,1,0:T(8,128)(2,1)S(1)} copy(bf16[8,8,256,128]{3,1,2,0:T(8,128)(2,1)S(1)} %fusion) | data formatting | bytes 8388608
  8.3 0.0 copy-done.1
  8.3 3.5 %fusion.1 = f32[256,64,64]{0,2,1:T(8,128)} fusion(bf16[256,128,64]{1,0,2:T(8,128)(2,1)S(1)} %bitcast.17, bf16[128,64]{0,1:T(8,128)(2,1)S(1)} %copy-done.1), kind=kOutput, calls=%fused_computation.2 | convolution fusion | flops 268435456 | bytes 8404992 | tf_op jit(solution)/shard_map/jr,ijs->sri/dot_general | solution.py:360
  11.8 65.7 %shard_map.37 = f32[16,256]{1,0:T(8,128)} custom-call(f32[2,2048,256]{2,1,0:T(8,128)} %bitcast.18), custom_call_target="tpu_custom_call" | custom-call | tf_op jit(solution)/shard_map/pallas_call | solution.py:322
  77.5 1.3 %multiply_bitcast_fusion = f32[256,16]{0,1:T(8,128)} fusion(f32[16,256]{1,0:T(8,128)} %shard_map.37), kind=kLoop, calls=%fused_computation.4 | loop fusion | flops 4096 | bytes 32768 | tf_op jit(solution)/shard_map/mul | solution.py:369
Async XLA Ops:
  0.0 0.7 copy-start
  7.1 1.2 %copy-start.1 = (bf16[128,64]{0,1:T(8,128)(2,1)S(1)}, bf16[128,64]{0,1:T(8,128)(2,1)}, u32[]{:S(2)}) copy-start(bf16[128,64]{0,1:T(8,128)(2,1)} %param.4) | copy-start | bytes 49156

commit v13 on v12

--- a/solution.py
+++ b/solution.py
@@ -76,7 +76,7 @@
     lax.fori_loop(1, n, finish, 0)
 
 
-def ring_flat(n, me, dev, x_ref, out_ref, recv, sendbuf, send_sem, recv_sem, blk, ready=None):
+def ring_flat(n, me, dev, x_ref, out_ref, recv, sendbuf, send_sem, recv_sem, blk, ready=None, lane_done=None):
     lanes = recv.shape[0]
     part = blk // lanes
     towards = (lax.rem(me + 1, n), lax.rem(me + n - 1, n))
@@ -104,6 +104,8 @@
                 copy(d, step + 1).start()
             else:
                 out_ref[pl.ds(d * part, part)] = total
+                if lane_done is not None:
+                    lane_done(d, part)
     for step in range(n - 1):
         for d in range(lanes):
             copy(d, step).wait_send()
@@ -226,11 +228,19 @@
         for k in range(len(firsts), n_y):
             core_finish(k)
 
-    ring_flat(n_y, me_y, y_dev, part_a, ring_a_out, ring_a_recv, ring_a_send, s_ra, r_ra, blk_a, ready=rest_ready)
+    depth_a = ring_a_out.shape[0] // n_ba
+
+    def send_lane(d, part):
+        for p in range(d * part // depth_a, (d + 1) * part // depth_a):
+            @pl.when(me_ba != p)
+            def _():
+                remote(ring_a_out.at[pl.ds(p * depth_a, depth_a)], z_a_recv.at[me_ba], s_za.at[p], r_za.at[me_ba],
+                       ba_dev(p)).start()
+
+    ring_flat(n_y, me_y, y_dev, part_a, ring_a_out, ring_a_recv, ring_a_send, s_ra, r_ra, blk_a, ready=rest_ready,
+              lane_done=send_lane)
     direct_finish(n_ba, me_ba, ba_dev, part_b, z_b_out, z_b_recv, s_zb, r_zb, blk_zb)
-    depth_a = ring_a_out.shape[0] // n_ba
     depth_b = blk_zb // n_y
-    direct_start(n_ba, me_ba, ba_dev, ring_a_out, z_a_recv, s_za, r_za, depth_a)
     ring_flat(n_y, me_y, y_dev, z_b_out, q_buf.at[pl.ds(depth_a, depth_b)], ring_b_recv, ring_b_send, s_rb, r_rb, depth_b)
     direct_finish(n_ba, me_ba, ba_dev, ring_a_out, q_buf.at[pl.ds(0, depth_a)], z_a_recv, s_za, r_za, depth_a)
 

time: 79.1 us -> 78.7 us (level)
  no operation moved by 1% of the time
where the time goes in v13:
time: 78.7 us; the launch traced here: 78.4 us
  Pallas kernels  65.3 us (83%)
  matrix products  9.9 us (13%)
  local copies, waits for them, and re-layouts  1.88 us (2%)
  other arithmetic  1.33 us (2%)
    pallas_call x1, Pallas kernels, reduce_and_gram(): pl.pallas_call(functools.partial(whole_kernel, sizes), out_shape=jax.Shap...  65.3 us
    dot_general x1, matrix products, project(): jnp.dot(tensor.reshape(local_rows * local_two, tensor.shape[2]), factor_t...  6.39 us
    dot_general x1, matrix products, project(): jnp.einsum('jr,ijs->sri', factor_two, partial_value, preferred_element_ty...  3.5 us
    unnamed x5, local copies, waits for them, and re-layouts  1.88 us

profile of v13, /device:TPU:1, one launch (start us, length us, event | category | flops | bytes accessed | tf_op | source)
XLA Modules:
  0.0 78.4 jit_solution(14694089909089289753)
XLA Ops:
  0.0 0.0 copy-start
  0.0 0.7 copy-done
  0.7 6.4 %fusion = bf16[8,8,256,128]{3,1,2,0:T(8,128)(2,1)S(1)} fusion(bf16[32768,128]{1,0:T(8,128)(2,1)} %bitcast.19, bf16[128,64]{0,1:T(8,128)(2,1)S(1)} %copy-done), kind=kOutput, calls=%fused_computation.1 | convolution fusion | flops 538968064 | bytes 12599296 | tf_op jit(solution)/shard_map/dot_general | solution.py:367
  7.1 0.0 copy-start.1
  7.1 1.2 %copy.4 = bf16[8,8,256,128]{3,2,1,0:T(8,128)(2,1)S(1)} copy(bf16[8,8,256,128]{3,1,2,0:T(8,128)(2,1)S(1)} %fusion) | data formatting | bytes 8388608
  8.3 0.0 copy-done.1
  8.3 3.5 %fusion.1 = f32[256,64,64]{0,2,1:T(8,128)} fusion(bf16[256,128,64]{1,0,2:T(8,128)(2,1)S(1)} %bitcast.17, bf16[128,64]{0,1:T(8,128)(2,1)S(1)} %copy-done.1), kind=kOutput, calls=%fused_computation.2 | convolution fusion | flops 268435456 | bytes 8404992 | tf_op jit(solution)/shard_map/jr,ijs->sri/dot_general | solution.py:370
  11.8 65.3 %shard_map.37 = f32[16,256]{1,0:T(8,128)} custom-call(f32[2,2048,256]{2,1,0:T(8,128)} %bitcast.18), custom_call_target="tpu_custom_call" | custom-call | tf_op jit(solution)/shard_map/pallas_call | solution.py:332
  77.1 1.3 %multiply_bitcast_fusion = f32[256,16]{0,1:T(8,128)} fusion(f32[16,256]{1,0:T(8,128)} %shard_map.37), kind=kLoop, calls=%fused_computation.4 | loop fusion | flops 4096 | bytes 32768 | tf_op jit(solution)/shard_map/mul | solution.py:379
Async XLA Ops:
  0.0 0.7 copy-start
  7.1 1.2 %copy-start.1 = (bf16[128,64]{0,1:T(8,128)(2,1)S(1)}, bf16[128,64]{0,1:T(8,128)(2,1)}, u32[]{:S(2)}) copy-start(bf16[128,64]{0,1:T(8,128)(2,1)} %param.4) | copy-start | bytes 49156

commit v14 on v13

--- a/solution.py
+++ b/solution.py
@@ -296,7 +296,9 @@
         c_out(c).start()
         return carry
 
-    lax.fori_loop(1, n_col, c_start, 0)
+    order = sorted(range(1, n_col), key=lambda k: -min(k, n_col - k))
+    for step in order:
+        c_start(step, 0)
     part[...] = term_block(me_col)
 
     def c_wait(step, carry):

time: 78.7 us -> 77.3 us (0.982)
  Pallas kernels: 65.3 us -> 63.9 us
    pallas_call x1, Pallas kernels: 65.3 us -> 63.9 us  [reduce_and_gram(): pl.pallas_call(functools.partial(whole_kernel, sizes), out_shape=jax.Shap...]
where the time goes in v14:
time: 77.3 us; the launch traced here: 77 us
  Pallas kernels  63.9 us (83%)
  matrix products  9.9 us (13%)
  local copies, waits for them, and re-layouts  1.88 us (2%)
  other arithmetic  1.33 us (2%)
    pallas_call x1, Pallas kernels, reduce_and_gram(): pl.pallas_call(functools.partial(whole_kernel, sizes), out_shape=jax.Shap...  63.9 us
    dot_general x1, matrix products, project(): jnp.dot(tensor.reshape(local_rows * local_two, tensor.shape[2]), factor_t...  6.39 us
    dot_general x1, matrix products, project(): jnp.einsum('jr,ijs->sri', factor_two, partial_value, preferred_element_ty...  3.5 us
    unnamed x5, local copies, waits for them, and re-layouts  1.88 us

profile of v14, /device:TPU:1, one launch (start us, length us, event | category | flops | bytes accessed | tf_op | source)
XLA Modules:
  0.0 77.0 jit_solution(7732602405448645496)
XLA Ops:
  0.0 0.0 copy-start
  0.0 0.7 copy-done
  0.7 6.4 %fusion = bf16[8,8,256,128]{3,1,2,0:T(8,128)(2,1)S(1)} fusion(bf16[32768,128]{1,0:T(8,128)(2,1)} %bitcast.19, bf16[128,64]{0,1:T(8,128)(2,1)S(1)} %copy-done), kind=kOutput, calls=%fused_computation.1 | convolution fusion | flops 538968064 | bytes 12599296 | tf_op jit(solution)/shard_map/dot_general | solution.py:369
  7.1 0.0 copy-start.1
  7.1 1.2 %copy.4 = bf16[8,8,256,128]{3,2,1,0:T(8,128)(2,1)S(1)} copy(bf16[8,8,256,128]{3,1,2,0:T(8,128)(2,1)S(1)} %fusion) | data formatting | bytes 8388608
  8.3 0.0 copy-done.1
  8.3 3.5 %fusion.1 = f32[256,64,64]{0,2,1:T(8,128)} fusion(bf16[256,128,64]{1,0,2:T(8,128)(2,1)S(1)} %bitcast.17, bf16[128,64]{0,1:T(8,128)(2,1)S(1)} %copy-done.1), kind=kOutput, calls=%fused_computation.2 | convolution fusion | flops 268435456 | bytes 8404992 | tf_op jit(solution)/shard_map/jr,ijs->sri/dot_general | solution.py:372
  11.8 63.9 %shard_map.37 = f32[16,256]{1,0:T(8,128)} custom-call(f32[2,2048,256]{2,1,0:T(8,128)} %bitcast.18), custom_call_target="tpu_custom_call" | custom-call | tf_op jit(solution)/shard_map/pallas_call | solution.py:334
  75.7 1.3 %multiply_bitcast_fusion = f32[256,16]{0,1:T(8,128)} fusion(f32[16,256]{1,0:T(8,128)} %shard_map.37), kind=kLoop, calls=%fused_computation.4 | loop fusion | flops 4096 | bytes 32768 | tf_op jit(solution)/shard_map/mul | solution.py:381
Async XLA Ops:
  0.0 0.7 copy-start
  7.1 1.2 %copy-start.1 = (bf16[128,64]{0,1:T(8,128)(2,1)S(1)}, bf16[128,64]{0,1:T(8,128)(2,1)}, u32[]{:S(2)}) copy-start(bf16[128,64]{0,1:T(8,128)(2,1)} %param.4) | copy-start | bytes 49156

commit v15 on v14

--- a/solution.py
+++ b/solution.py
@@ -30,7 +30,8 @@
         outgoing(lax.rem(me + step, n)).start()
         return carry
 
-    lax.fori_loop(1, n, start, 0)
+    for step in sorted(range(1, n), key=lambda k: -min(k, n - k)):
+        start(step, 0)
     out_ref[...] = piece(me)[...]
 
     def gather(step, carry):
@@ -54,7 +55,8 @@
         remote(x_ref.at[pl.ds(peer * blk, blk)], recv.at[me], send_sem.at[peer], recv_sem.at[me], dev(peer)).start()
         return carry
 
-    lax.fori_loop(1, n, start, 0)
+    for step in sorted(range(1, n), key=lambda k: -min(k, n - k)):
+        start(step, 0)
 
 
 def direct_finish(n, me, dev, x_ref, out_ref, recv, send_sem, recv_sem, blk):

time: 77.3 us -> 77.2 us (level)
  no operation moved by 1% of the time
where the time goes in v15:
time: 77.2 us; the launch traced here: 76.8 us
  Pallas kernels  63.6 us (82%)
  matrix products  9.9 us (13%)
  local copies, waits for them, and re-layouts  1.88 us (2%)
  other arithmetic  1.33 us (2%)
    pallas_call x1, Pallas kernels, reduce_and_gram(): pl.pallas_call(functools.partial(whole_kernel, sizes), out_shape=jax.Shap...  63.6 us
    dot_general x1, matrix products, project(): jnp.dot(tensor.reshape(local_rows * local_two, tensor.shape[2]), factor_t...  6.39 us
    dot_general x1, matrix products, project(): jnp.einsum('jr,ijs->sri', factor_two, partial_value, preferred_element_ty...  3.5 us
    unnamed x5, local copies, waits for them, and re-layouts  1.88 us

profile of v15, /device:TPU:1, one launch (start us, length us, event | category | flops | bytes accessed | tf_op | source)
XLA Modules:
  0.0 76.8 jit_solution(11988240114337260920)
XLA Ops:
  0.0 0.0 copy-start
  0.0 0.7 copy-done
  0.7 6.4 %fusion = bf16[8,8,256,128]{3,1,2,0:T(8,128)(2,1)S(1)} fusion(bf16[32768,128]{1,0:T(8,128)(2,1)} %bitcast.19, bf16[128,64]{0,1:T(8,128)(2,1)S(1)} %copy-done), kind=kOutput, calls=%fused_computation.1 | convolution fusion | flops 538968064 | bytes 12599296 | tf_op jit(solution)/shard_map/dot_general | solution.py:371
  7.1 0.0 copy-start.1
  7.1 1.2 %copy.4 = bf16[8,8,256,128]{3,2,1,0:T(8,128)(2,1)S(1)} copy(bf16[8,8,256,128]{3,1,2,0:T(8,128)(2,1)S(1)} %fusion) | data formatting | bytes 8388608
  8.3 0.0 copy-done.1
  8.3 3.5 %fusion.1 = f32[256,64,64]{0,2,1:T(8,128)} fusion(bf16[256,128,64]{1,0,2:T(8,128)(2,1)S(1)} %bitcast.17, bf16[128,64]{0,1:T(8,128)(2,1)S(1)} %copy-done.1), kind=kOutput, calls=%fused_computation.2 | convolution fusion | flops 268435456 | bytes 8404992 | tf_op jit(solution)/shard_map/jr,ijs->sri/dot_general | solution.py:374
  11.8 63.6 %shard_map.37 = f32[16,256]{1,0:T(8,128)} custom-call(f32[2,2048,256]{2,1,0:T(8,128)} %bitcast.18), custom_call_target="tpu_custom_call" | custom-call | tf_op jit(solution)/shard_map/pallas_call | solution.py:336
  75.5 1.3 %multiply_bitcast_fusion = f32[256,16]{0,1:T(8,128)} fusion(f32[16,256]{1,0:T(8,128)} %shard_map.37), kind=kLoop, calls=%fused_computation.4 | loop fusion | flops 4096 | bytes 32768 | tf_op jit(solution)/shard_map/mul | solution.py:383
Async XLA Ops:
  0.0 0.7 copy-start
  7.1 1.2 %copy-start.1 = (bf16[128,64]{0,1:T(8,128)(2,1)S(1)}, bf16[128,64]{0,1:T(8,128)(2,1)}, u32[]{:S(2)}) copy-start(bf16[128,64]{0,1:T(8,128)(2,1)} %param.4) | copy-start | bytes 49156
